TPU v7x, 256 devices: a whole 4x4x8 slice. The times are simulated.
256 devices in a mesh: et: 16 (over y, x), ex: 8 (over z), dp: 2 (over core).
Axes of the slice: x: 4, y: 4, z: 8, core: 2. Of those that a mesh axis runs over, the one named last changes fastest.
Arguments:
- tokens: bfloat16 [8192, 1664], P(('et', 'ex', 'dp')), may hold values from -6 to 6
- gate_probs: float32 [8192, 2], P(('et', 'ex', 'dp')), may hold values from 0.2 to 1
- expert_ids: int32 [8192, 2], P(('et', 'ex', 'dp')), may hold values from 0 to 15, as said below
- copies: int32 [16], replicated, may hold values from 1 to 2, as said below
- weight_in: bfloat16 [16, 1664, 8192], P('ex', None, ('et', 'dp')), may hold values from -0.15625 to 0.15625
- weight_out: bfloat16 [16, 8192, 1664], P('ex', ('et', 'dp')), may hold values from -0.0625 to 0.0625
- cotangent: bfloat16 [8192, 1664], P(('et', 'ex', 'dp')), may hold values from -6 to 6
Outputs:
- layer_out: bfloat16 [8192, 1664], P(('et', 'ex', 'dp'))
- grad_tokens: bfloat16 [8192, 1664], P(('et', 'ex', 'dp'))
- grad_gates: float32 [8192, 2], P(('et', 'ex', 'dp'))
- grad_weight_in: float32 [16, 1664, 8192], P('ex', None, ('et', 'dp'))
- grad_weight_out: float32 [16, 8192, 1664], P('ex', ('et', 'dp'))
Inputs may be any that keep to these rules, and one draw needn't show every extreme that they name: `expert_ids`: the two experts of a token differ. Of each aligned run of 2 experts exactly one has 2 copies.
All inputs are finite; a program needn't handle non-finite values.
Results may differ from a plain program's by a relative error of at most 0.02.
Values may be sent and summed in bfloat16 or wider, within the bound.
A program may use at most 128 MiB of HBM per device.

v0:
```python
import jax
import jax.numpy as jnp
from jax import lax
from jax.sharding import Mesh
from jax.sharding import PartitionSpec as P

ET = ("et_0", "et_1")
ET_EX_DP = ("et_0", "et_1", "ex", "dp")
ET_DP = ("et_0", "et_1", "dp")


gelu_scale = 0.7978845608028654


def sent_together(arrays, axis, dim, along):
    ends, at = ([], 0)
    for a in arrays[:-1]:
        at += a.shape[along]
        ends.append(at)
    both = jnp.concatenate(arrays, axis=along)
    return tuple(jnp.split(lax.all_gather(both, axis, axis=dim, tiled=True), ends, axis=along))


def scatter_axes(shard, axes, dim):
    for axis in axes:
        shard = lax.psum_scatter(shard, axis, scatter_dimension=dim, tiled=True)
    return shard


def in_one_piece(arrays, axis, split_dim, concat_dim, along):
    widths = [a.shape[along] for a in arrays]
    both = jnp.concatenate(arrays, axis=along)
    result = lax.all_to_all(both, axis, split_axis=split_dim, concat_axis=concat_dim, tiled=True)
    return tuple(jnp.split(result, [sum(widths[:k]) for k in range(1, len(widths))], axis=along))


def turned_gather(arrays, axis, dims):
    turned = [jnp.moveaxis(a, dim, 0) for a, dim in zip(arrays, dims)]
    both = jnp.concatenate([t.reshape(len(t), -1) for t in turned], axis=1)
    result, at, outs = (lax.all_gather(both, axis, axis=0, tiled=True), 0, [])
    for t, dim in zip(turned, dims):
        share = result[:, at : at + t[0].size].reshape(-1, *t.shape[1:])
        outs.append(jnp.moveaxis(share, 0, dim))
        at += t[0].size
    return tuple(outs)


def split_up(shard, dim, peers):
    lengths = shard.shape
    blocks = shard.reshape(*lengths[:dim], peers, lengths[dim] // peers, *lengths[dim + 1 :])
    return jnp.moveaxis(blocks, dim, 0)


def sum_at_owner(shard, axis, dim):
    blocks = split_up(shard, dim, lax.axis_size(axis))
    arrived = lax.all_to_all(blocks, axis, split_axis=0, concat_axis=0, tiled=True)
    return arrived.astype(jnp.float32).sum(axis=0)


def gelu_tanh(values):
    inner_arg = gelu_scale * (values + 0.044715 * values * values * values)
    return 0.5 * values * (1.0 + jnp.tanh(inner_arg))


def gelu_slope(values):
    return jax.jvp(gelu_tanh, (values,), (jnp.ones_like(values),))[1]


def rounded(values):
    narrow = lax.optimization_barrier(values.astype(jnp.bfloat16))
    return narrow.astype(jnp.float32)


def slot_table(expert_ids, copies, capacity, group_size):
    experts = copies.shape[0]
    flat_ids = expert_ids.reshape(-1)
    labels = jnp.arange(experts, dtype=jnp.int32)
    onehot = (flat_ids[:, None] == labels[None, :]).astype(jnp.int32)
    earlier = jnp.cumsum(onehot, axis=0) - onehot
    ranking = jnp.sum(earlier * onehot, axis=1)
    allowed = capacity * jnp.sum(onehot * copies[None, :], axis=1)
    owner_group = flat_ids // group_size
    within = flat_ids % group_size
    per_group = group_size * capacity + capacity
    offset = jnp.where(
        ranking < capacity, within * capacity + ranking, group_size * capacity + ranking - capacity
    )
    target = jnp.where(ranking < allowed, owner_group * per_group + offset, -1)
    columns = jnp.arange(experts // group_size * per_group, dtype=jnp.int32)
    return ((target[:, None] == columns[None, :]).astype(jnp.bfloat16), per_group)


def expert_forward(row_block, weight_in, weight_out, portions):
    pre_act = jnp.einsum(
        "arsjcd,jdf->arsjcf", row_block, weight_in, preferred_element_type=jnp.float32
    )
    hidden = gelu_tanh(pre_act).astype(jnp.bfloat16)
    part_width = hidden.shape[-1] // portions
    blocks = hidden.reshape(hidden.shape[:-1] + (portions, part_width))
    weight_parts = weight_out.reshape(
        (weight_out.shape[0], portions, part_width, weight_out.shape[-1])
    )
    partials = jnp.einsum(
        "arsjcbf,jbfd->arsjcbd", blocks, weight_parts, preferred_element_type=jnp.float32
    )
    return (jnp.sum(rounded(partials), axis=5), pre_act, hidden)


def expert_backward(row_block, up_block, pre_act, hidden, weight_in, weight_out, portions):
    back_hidden = jnp.einsum(
        "arsjcd,jfd->arsjcf", up_block, weight_out, preferred_element_type=jnp.float32
    )
    slope_rows = (back_hidden * gelu_slope(pre_act)).astype(jnp.bfloat16)
    grad_out = jnp.einsum(
        "arsjcf,arsjcd->rjfd", hidden, up_block, preferred_element_type=jnp.float32
    )
    grad_in = jnp.einsum(
        "arsjcd,arsjcf->rjdf", row_block, slope_rows, preferred_element_type=jnp.float32
    )
    part_width = slope_rows.shape[-1] // portions
    blocks = slope_rows.reshape(slope_rows.shape[:-1] + (portions, part_width))
    weight_parts = weight_in.reshape((weight_in.shape[0], weight_in.shape[1], portions, part_width))
    partials = jnp.einsum(
        "arsjcbf,jdbf->arsjcbd", blocks, weight_parts, preferred_element_type=jnp.float32
    )
    return (jnp.sum(rounded(partials), axis=5), grad_in, grad_out)


def spread_slots(inputs, upstream):
    spread = sent_together((inputs[None], upstream[None]), ET, 0, 1)
    return spread


def settle_slots(term):
    summed = scatter_axes(term.astype(jnp.bfloat16), ET, 0).astype(jnp.float32)
    narrow = summed[0].astype(jnp.bfloat16)
    return lax.all_to_all(narrow, "ex", split_axis=0, concat_axis=0, tiled=True)


def shards(tokens, gate_probs, expert_ids, copies, weight_in, weight_out, cotangent):
    experts = copies.shape[0]
    model_width = tokens.shape[1]
    group_count = lax.axis_size("ex")
    group_size = experts // group_count
    capacity = max(2, tokens.shape[0] // 16)
    routing, per_group = slot_table(expert_ids, copies, capacity, group_size)
    token_rows = jnp.repeat(tokens, 2, axis=0)
    upstream = (
        gate_probs.reshape(-1, 1) * jnp.repeat(cotangent, 2, axis=0).astype(jnp.float32)
    ).astype(jnp.bfloat16)
    sent_inputs = jnp.dot(routing.T, token_rows, preferred_element_type=jnp.float32).astype(
        jnp.bfloat16
    )
    sent_upstream = jnp.dot(routing.T, upstream, preferred_element_type=jnp.float32).astype(
        jnp.bfloat16
    )
    frame_shape = (group_count, per_group, model_width)
    arrived = in_one_piece(
        (sent_inputs.reshape(frame_shape), sent_upstream.reshape(frame_shape)), "ex", 0, 0, 1
    )
    full_in, full_out = turned_gather((weight_in, weight_out), "dp", (2, 1))
    portions = full_in.shape[2] // weight_in.shape[2]
    spread_in, spread_up = spread_slots(arrived[0], arrived[1])
    tensor = lax.axis_size(ET)
    replicas = spread_in.shape[0] // tensor
    row_frame = (tensor, replicas, group_count, per_group, model_width)
    rows_all = spread_in.reshape(row_frame)
    up_all = spread_up.reshape(row_frame)
    base_cols = group_size * capacity
    local_copies = lax.dynamic_slice_in_dim(
        copies, lax.axis_index("ex") * group_size, group_size, 0
    )
    doubled = jnp.sum(
        jnp.arange(group_size, dtype=jnp.int32) * (local_copies == 2).astype(jnp.int32)
    )
    base_shape = (tensor, replicas, group_count, group_size, capacity, model_width)
    extra_shape = (tensor, replicas, group_count, 1, capacity, model_width)
    pieces = [
        (
            rows_all[:, :, :, :base_cols].reshape(base_shape),
            up_all[:, :, :, :base_cols].reshape(base_shape),
            full_in,
            full_out,
        ),
        (
            rows_all[:, :, :, base_cols:].reshape(extra_shape),
            up_all[:, :, :, base_cols:].reshape(extra_shape),
            lax.dynamic_slice_in_dim(full_in, doubled, 1, 0),
            lax.dynamic_slice_in_dim(full_out, doubled, 1, 0),
        ),
    ]
    outputs = []
    input_grads = []
    grads_in = []
    grads_out = []
    for row_block, up_block, piece_in, piece_out in pieces:
        result, pre_act, hidden = expert_forward(row_block, piece_in, piece_out, portions)
        back_rows, grad_in, grad_out = expert_backward(
            row_block, up_block, pre_act, hidden, piece_in, piece_out, portions
        )
        outputs.append(result.reshape(tensor * replicas, group_count, -1, model_width))
        input_grads.append(back_rows.reshape(tensor * replicas, group_count, -1, model_width))
        grads_in.append(grad_in)
        grads_out.append(grad_out)
    returned = settle_slots(jnp.concatenate(outputs, axis=2))
    grad_in = grads_in[0]
    grad_out = grads_out[0]
    grad_in = lax.dynamic_update_slice_in_dim(
        grad_in, lax.dynamic_slice_in_dim(grad_in, doubled, 1, 1) + grads_in[1], doubled, 1
    )
    grad_out = lax.dynamic_update_slice_in_dim(
        grad_out, lax.dynamic_slice_in_dim(grad_out, doubled, 1, 1) + grads_out[1], doubled, 1
    )
    part_in = jnp.sum(rounded(grad_in), axis=0)
    part_out = jnp.sum(rounded(grad_out), axis=0)
    grad_weight_in, grad_weight_out = (
        sum_at_owner(part_in.astype(jnp.bfloat16), "dp", 2),
        sum_at_owner(part_out.astype(jnp.bfloat16), "dp", 1),
    )
    back_slots = settle_slots(jnp.concatenate(input_grads, axis=2))
    expert_out = jnp.dot(
        routing, returned.reshape(-1, model_width), preferred_element_type=jnp.float32
    )
    gate_pairs = expert_out.reshape(-1, 2, model_width)
    layer_out = jnp.sum(gate_probs[:, :, None] * gate_pairs, axis=1).astype(jnp.bfloat16)
    grad_gates = jnp.sum(cotangent.astype(jnp.float32)[:, None, :] * gate_pairs, axis=2)
    grad_rows = jnp.dot(
        routing, back_slots.reshape(-1, model_width), preferred_element_type=jnp.float32
    )
    grad_tokens = jnp.sum(grad_rows.reshape(-1, 2, model_width), axis=1).astype(jnp.bfloat16)
    return (layer_out, grad_tokens, grad_gates, grad_weight_in, grad_weight_out)


def solution(mesh):
    torus = Mesh(
        mesh.devices.reshape(4, 4, mesh.shape["ex"], mesh.shape["dp"]), ("et_0", "et_1", "ex", "dp")
    )
    placed = (
        P(ET_EX_DP, None),
        P(ET_EX_DP, None),
        P(ET_EX_DP, None),
        P(),
        P("ex", None, ET_DP),
        P("ex", ET_DP, None),
        P(ET_EX_DP, None),
    )
    return jax.shard_map(
        shards,
        mesh=torus,
        in_specs=placed,
        out_specs=(
            P(ET_EX_DP, None),
            P(ET_EX_DP, None),
            P(ET_EX_DP, None),
            P("ex", None, ET_DP),
            P("ex", ET_DP, None),
        ),
        check_vma=False,
    )
```

profile of v0, /device:TPU:8, one launch (start us, length us, event | category | flops | bytes accessed | tf_op | source)
XLA Modules:
  0.0 293.9 jit_solution(14587058970957887210)
XLA Ops:
  15.4 23.6 %all_to_all.25 = bf16[8,12,1664]{2,1,0:T(8,128)(2,1)S(1)} all-to-all(bf16[8,12,1664]{2,1,0:T(8,128)(2,1)S(1)} %pad_maximum_fusion.3), channel_id=1, replica_groups=mesh['et_0'=4,'et_1'=4,'ex'=8,'dp'=2] {'ex'}, dimensions={0} | all-to-all | bytes 638976 | tf_op jit(solution)/shard_map/all_to_all | solution.py:33
  42.7 5.2 %fusion.109 = (bf16[512,3328]{0,1:T(8,128)(2,1)S(1)}, bf16[512,3328]{0,1:T(8,128)(2,1)}) fusion(bf16[512,6656]{0,1:T(8,128)(2,1)} %all-gather.3.cloned.1.call-done), kind=kLoop, calls=%fused_computation.140 | loop fusion | bytes 13631488 | tf_op jit(solution)/shard_map/slice | solution.py:42
  47.9 5.5 %copy.180 = bf16[512,2,1664]{2,0,1:T(8,128)(2,1)} copy(bf16[512,2,1664]{0,2,1:T(8,128)(2,1)} %bitcast.233) | data formatting | bytes 6815744 | tf_op jit(solution)/shard_map/reshape | solution.py:42
  53.4 3.7 %dynamic-slice_bitcast_fusion = (bf16[1,1664,512]{2,1,0:T(8,128)(2,1)}, bf16[512,1,1664]{0,2,1:T(8,128)(2,1)}) fusion(bf16[512,2,1664]{0,2,1:T(8,128)(2,1)S(1)} %bitcast.229, s32[]{:T(128)S(6)} %select_n.67, bf16[512,2,1664]{0,2,1:T(8,128)(2,1)} %bitcast.234), kind=kLoop, calls=%fused_computation.41 | loop fusion | bytes 6815748 | tf_op jit(solution)/shard_map/dynamic_slice | solution.py:188
  57.1 4.7 %reshape.314 = bf16[1664,2,256]{2,1,0:T(2,128)(2,1)} reshape(bf16[1,1664,512]{2,1,0:T(8,128)(2,1)} %get-tuple-element.21) | data formatting | bytes 3407872 | tf_op jit(solution)/shard_map/reshape.18
  64.3 37.2 %all-gather.5.cloned.1.call-done = bf16[16,16,6,1664]{3,1,2,0:T(8,128)(2,1)} async-done(((bf16[1,16,6,1664]{3,1,2,0:T(8,128)(2,1)}), bf16[16,16,6,1664]{3,1,2,0:T(8,128)(2,1)}) %all-gather.5.cloned.1.call-update) | async-done | bytes 5111824 | tf_op jit(solution)/shard_map/all_gather | solution.py:21
  113.5 3.4 %fusion.12 = bf16[16,1,8,1,2,2,1664]{6,0,4,2,5,1,3:T(8,128)(2,1)} fusion(bf16[1664,2,256,1,1]{2,1,0,4,3:T(2,128)(2,1)} %bitcast.245, bf16[16,8,2,2,256]{4,3,0,2,1:T(2,128)(2,1)} %reshape.317), kind=kOutput, calls=%fused_computation.21 | convolution fusion | flops 437059584 | bytes 3670016 | tf_op jit(solution)/shard_map/arsjcbf,jdbf->arsjcbd/dot_general | solution.py:123
  122.1 3.8 %fusion.61 = (bf16[16,1,8,2,2,512]{5,0,4,2,3,1:T(8,128)(2,1)}, f32[16,1,8,2,2,512]{5,0,4,2,3,1:T(8,128)S(1)}) fusion(bf16[2,1664,512,1,1]{2,1,4,3,0:T(8,128)(2,1)S(1)} %bitcast.232, bf16[16,8,2,2,1664]{4,0,3,2,1:T(8,128)(2,1)} %bitcast.252), kind=kOutput, calls=%fused_computation.60 | convolution fusion | flops 874774528 | bytes 6684672 | tf_op jit(solution)/shard_map/arsjcd,jdf->arsjcf/dot_general | solution.py:94
  130.2 4.0 %fusion.7 = bf16[16,1,8,2,2,2,1664]{6,0,4,2,5,3,1:T(8,128)(2,1)} fusion(bf16[2,1664,2,256,1,1]{3,2,1,0,5,4:T(2,128)(2,1)S(1)} %bitcast.235, bf16[16,8,2,2,2,256]{5,4,0,3,1,2:T(2,128)(2,1)} %reshape.312), kind=kOutput, calls=%fused_computation.16 | convolution fusion | flops 874119168 | bytes 7340032 | tf_op jit(solution)/shard_map/arsjcbf,jdbf->arsjcbd/dot_general | solution.py:123
  146.3 4.8 %fusion.10 = bf16[16,1,8,2,2,2,1664]{6,0,4,2,5,3,1:T(8,128)(2,1)} fusion(bf16[2,2,256,1664,1,1]{3,2,5,4,1,0:T(8,128)(2,1)} %bitcast.254, bf16[16,8,2,2,2,256]{5,4,0,3,1,2:T(2,128)(2,1)S(1)} %reshape.302), kind=kOutput, calls=%fused_computation.17 | convolution fusion | flops 874119168 | bytes 7340032 | tf_op jit(solution)/shard_map/arsjcbf,jbfd->arsjcbd/dot_general | solution.py:103
  165.3 8.8 %reduce-scatter.9.cloned.1.call-done = bf16[4,8,6,1664]{3,1,2,0:T(8,128)(2,1)} async-done(((bf16[16,8,6,1664]{3,1,2,0:T(8,128)(2,1)}), bf16[4,8,6,1664]{3,1,2,0:T(8,128)(2,1)}) %reduce-scatter.9.cloned.1.call-update) | async-done | bytes 638992 | tf_op jit(solution)/shard_map/reduce_scatter | solution.py:26
  174.2 3.9 %fusion.73 = f32[2,512,1664,1,1]{2,1,3,0,4:T(8,128)} fusion(bf16[16,8,2,2,1664]{4,0,3,2,1:T(8,128)(2,1)S(1)} %bitcast.256, bf16[16,1,8,2,2,512]{5,0,4,2,3,1:T(8,128)(2,1)S(1)} %copy-done.12), kind=kOutput, calls=%fused_computation.77 | convolution fusion | flops 872415232 | bytes 9043968 | tf_op jit(solution)/shard_map/arsjcf,arsjcd->rjfd/dot_general | solution.py:114
  178.1 35.0 %reduce-scatter.5.cloned.1.call-done = bf16[4,8,6,1664]{3,1,2,0:T(8,128)(2,1)} async-done(((bf16[16,8,6,1664]{3,1,2,0:T(8,128)(2,1)}), bf16[4,8,6,1664]{3,1,2,0:T(8,128)(2,1)}) %reduce-scatter.5.cloned.1.call-update) | async-done | bytes 638992 | tf_op jit(solution)/shard_map/reduce_scatter | solution.py:26
  213.1 4.6 %fusion.3 = f32[1,2,1664,512]{3,2,1,0:T(8,128)} fusion(f32[1,2,1664,512]{3,2,1,0:T(8,128)} %copy.286, s32[]{:T(128)S(6)} %select_n.67, f32[2,1664,512]{2,1,0:T(8,128)} %bitcast.249, bf16[16,1,8,6,1664]{4,0,3,2,1:T(8,128)(2,1)} %bitcast.244, bf16[16,1,8,1,2,512]{5,0,4,2,1,3:T(8,128)(2,1)S(1)} %copy-done.16), kind=kOutput, calls=%fused_computation.10 | convolution fusion | flops 437059584 | bytes 7929860 | tf_op jit(solution)/shard_map/arsjcd,arsjcf->rjdf/dot_general | solution.py:117
  217.7 3.4 %convert_element_type.154 = bf16[1,2,1664,512]{3,2,1,0:T(8,128)(2,1)S(1)} convert(f32[1,2,1664,512]{3,2,1,0:T(8,128)} %fusion.3) | non-fusion elementwise | flops 1703936 | bytes 10223616 | tf_op jit(solution)/shard_map/convert_element_type | solution.py:70
  223.6 4.2 %copy.283 = bf16[2,1664,2,256]{3,1,0,2:T(8,128)(2,1)} copy(bf16[2,1664,2,256]{3,2,1,0:T(2,128)(2,1)} %convert_element_type.155) | data formatting | bytes 6815744 | tf_op jit(solution)/shard_map/convert_element_type | solution.py:217
  227.7 4.0 %all-to-all-start.3 = ((bf16[2,2,1664,256]{3,2,1,0:T(8,128)(2,1)}), bf16[2,2,1664,256]{3,2,1,0:T(8,128)(2,1)S(1)}, u32[]{:S(2)}, u32[]{:S(2)}) async-start(bf16[2,2,1664,256]{3,2,1,0:T(8,128)(2,1)} %bitcast.237), calls=%async_computation.7 | async-start | bytes 6815744 | tf_op jit(solution)/shard_map/all_to_all | solution.py:56
  231.8 3.1 %copy.287 = f32[1,2,512,1664]{3,2,1,0:T(8,128)S(1)} copy(f32[1,2,512,1664]{3,2,1,0:T(8,128)} %bitcast.250) | data formatting | bytes 13631488
  242.4 10.6 %all_to_all.26 = bf16[2,2,256,1664]{3,2,1,0:T(8,128)(2,1)} all-to-all(bf16[2,2,256,1664]{3,2,1,0:T(8,128)(2,1)} %bitcast.238), channel_id=1, replica_groups=mesh['et_0'=4,'et_1'=4,'ex'=8,'dp'=2] {'dp'}, dimensions={0} | all-to-all | bytes 6815744 | tf_op jit(solution)/shard_map/all_to_all | solution.py:56
  253.1 7.0 %all-to-all-start.2 = ((bf16[8,6,1664]{2,1,0:T(8,128)(2,1)}), bf16[8,6,1664]{2,1,0:T(8,128)(2,1)}, u32[]{:S(2)}, u32[]{:S(2)}) async-start(bf16[8,6,1664]{2,1,0:T(8,128)(2,1)} %copy.204), calls=%async_computation.6 | async-start | bytes 425984 | tf_op jit(solution)/shard_map/all_to_all | solution.py:137
  262.4 5.1 %reduce-scatter.7.cloned.1.call-done = bf16[1,8,6,1664]{3,1,2,0:T(8,128)(2,1)} async-done(((bf16[4,8,6,1664]{3,1,2,0:T(8,128)(2,1)}), bf16[1,8,6,1664]{3,1,2,0:T(8,128)(2,1)}) %reduce-scatter.7.cloned.1.call-update) | async-done | bytes 159760 | tf_op jit(solution)/shard_map/reduce_scatter | solution.py:26
  271.3 4.7 %all-to-all-start.1 = ((bf16[8,6,1664]{2,1,0:T(8,128)(2,1)}), bf16[8,6,1664]{2,1,0:T(8,128)(2,1)S(1)}, u32[]{:S(2)}, u32[]{:S(2)}) async-start(bf16[8,6,1664]{2,1,0:T(8,128)(2,1)} %copy.193), calls=%async_computation.3 | async-start | bytes 425984 | tf_op jit(solution)/shard_map/all_to_all | solution.py:137
  276.1 4.6 %convert_reduce_fusion = f32[2,256,1664]{2,1,0:T(8,128)} fusion(bf16[2,2,256,1664]{3,2,1,0:T(8,128)(2,1)} %all_to_all.26), kind=kLoop, calls=%fused_computation | loop fusion | flops 2555904 | bytes 6815744 | tf_op jit(solution)/shard_map/reduce_sum | solution.py:57
  282.5 3.5 %all-to-all-done.1 = bf16[8,6,1664]{2,1,0:T(8,128)(2,1)S(1)} async-done(((bf16[8,6,1664]{2,1,0:T(8,128)(2,1)}), bf16[8,6,1664]{2,1,0:T(8,128)(2,1)S(1)}, u32[]{:S(2)}, u32[]{:S(2)}) %all-to-all-start.1) | async-done | bytes 159776 | tf_op jit(solution)/shard_map/all_to_all | solution.py:137
  (129 shorter events, 79.2 us)
Async XLA Ops:
  7.2 3.0 %copy-start.11 = (bf16[2,1664,256]{2,1,0:T(8,128)(2,1)S(1)}, bf16[2,1664,256]{2,1,0:T(8,128)(2,1)}, u32[]{:S(2)}) copy-start(bf16[2,1664,256]{2,1,0:T(8,128)(2,1)} %param.11) | copy-start | bytes 5111812
  7.2 35.5 %all-gather.3.cloned.1.call-start = ((), (), s32[]{:S(2)}) async-start(), calls=%async_computation.9 | async-start | bytes 10223616 | tf_op jit(solution)/shard_map/all_gather | solution.py:40
  12.2 2.5 copy-start.18
  12.2 89.2 %all-gather.5.cloned.1.call-start = ((), (), s32[]{:S(2)}) async-start(), calls=%async_computation.10 | async-start | bytes 5431296 | tf_op jit(solution)/shard_map/all_gather | solution.py:21
  39.9 134.2 %reduce-scatter.9.cloned.1.call-start = ((), (), s32[]{:S(2)}) async-start(), calls=%async_computation.13 | async-start | bytes 3194880 | tf_op jit(solution)/shard_map/reduce_scatter | solution.py:26
  107.7 2.5 copy-start.5
  122.1 3.8 %copy-start.8 = (bf16[512,2,1664]{2,0,1:T(8,128)(2,1)S(1)}, bf16[512,2,1664]{2,0,1:T(8,128)(2,1)}, u32[]{:S(2)}) copy-start(bf16[512,2,1664]{2,0,1:T(8,128)(2,1)} %copy.180) | copy-start | bytes 10223620
  122.1 3.8 %copy-start.9 = (bf16[16,1,8,4,1664]{4,0,3,2,1:T(8,128)(2,1)S(1)}, bf16[16,1,8,4,1664]{4,0,3,2,1:T(8,128)(2,1)}, u32[]{:S(2)}) copy-start(bf16[16,1,8,4,1664]{4,0,3,2,1:T(8,128)(2,1)} %slice.28) | copy-start | bytes 5111812
  125.9 4.3 %copy-start = (bf16[2,1664,2,256]{3,2,1,0:T(2,128)(2,1)S(1)}, bf16[2,1664,2,256]{3,2,1,0:T(2,128)(2,1)}, u32[]{:S(2)}) copy-start(bf16[2,1664,2,256]{3,2,1,0:T(2,128)(2,1)} %reshape.309) | copy-start | bytes 10223620
  134.1 3.5 %copy-start.7 = (bf16[16,8,2,1664]{3,1,2,0:T(8,128)(2,1)S(1)}, bf16[16,8,2,1664]{3,1,2,0:T(8,128)(2,1)}, u32[]{:S(2)}) copy-start(bf16[16,8,2,1664]{3,1,2,0:T(8,128)(2,1)} %copy.203) | copy-start | bytes 2555908
  139.4 73.6 %reduce-scatter.5.cloned.1.call-start = ((), (), s32[]{:S(2)}) async-start(), calls=%async_computation.11 | async-start | bytes 3194880 | tf_op jit(solution)/shard_map/reduce_scatter | solution.py:26
  143.9 2.2 copy-start.12
  154.6 2.8 copy-start.4
  156.3 84.5 %reduce-scatter.11.cloned.1.call-start = ((), (), s32[]{:S(2)}) async-start(), calls=%async_computation.14 | async-start | bytes 798720 | tf_op jit(solution)/shard_map/reduce_scatter | solution.py:26
  159.6 2.8 copy-start.3
  162.4 11.8 %copy-start.10 = (bf16[16,1,8,4,1664]{4,0,3,2,1:T(8,128)(2,1)S(1)}, bf16[16,1,8,4,1664]{4,0,3,2,1:T(8,128)(2,1)}, u32[]{:S(2)}) copy-start(bf16[16,1,8,4,1664]{4,0,3,2,1:T(8,128)(2,1)} %slice.28) | copy-start | bytes 5111812
  174.1 39.0 %copy-start.16 = (bf16[16,1,8,1,2,512]{5,0,4,2,1,3:T(8,128)(2,1)S(1)}, bf16[16,1,8,1,2,512]{5,0,4,2,1,3:T(8,128)(2,1)}, u32[]{:S(2)}) copy-start(bf16[16,1,8,1,2,512]{5,0,4,2,1,3:T(8,128)(2,1)} %fusion.51) | copy-start | bytes 786436
  174.1 93.3 %reduce-scatter.7.cloned.1.call-start = ((), (), s32[]{:S(2)}) async-start(), calls=%async_computation.12 | async-start | bytes 798720 | tf_op jit(solution)/shard_map/reduce_scatter | solution.py:26
  227.7 14.7 %all-to-all-start.3 = ((bf16[2,2,1664,256]{3,2,1,0:T(8,128)(2,1)}), bf16[2,2,1664,256]{3,2,1,0:T(8,128)(2,1)S(1)}, u32[]{:S(2)}, u32[]{:S(2)}) async-start(bf16[2,2,1664,256]{3,2,1,0:T(8,128)(2,1)} %bitcast.237), calls=%async_computation.7 | async-start | bytes 6815744 | tf_op jit(solution)/shard_map/all_to_all | solution.py:56
  231.7 3.1 %copy-start.15 = (bf16[16,1,8,1,2,512]{5,0,4,2,1,3:T(8,128)(2,1)S(1)}, bf16[16,1,8,1,2,512]{5,0,4,2,1,3:T(8,128)(2,1)}, u32[]{:S(2)}) copy-start(bf16[16,1,8,1,2,512]{5,0,4,2,1,3:T(8,128)(2,1)} %get-tuple-element.17) | copy-start | bytes 786436
  253.1 18.3 %all-to-all-start.2 = ((bf16[8,6,1664]{2,1,0:T(8,128)(2,1)}), bf16[8,6,1664]{2,1,0:T(8,128)(2,1)}, u32[]{:S(2)}, u32[]{:S(2)}) async-start(bf16[8,6,1664]{2,1,0:T(8,128)(2,1)} %copy.204), calls=%async_computation.6 | async-start | bytes 425984 | tf_op jit(solution)/shard_map/all_to_all | solution.py:137
  271.3 14.7 %all-to-all-start.1 = ((bf16[8,6,1664]{2,1,0:T(8,128)(2,1)}), bf16[8,6,1664]{2,1,0:T(8,128)(2,1)S(1)}, u32[]{:S(2)}, u32[]{:S(2)}) async-start(bf16[8,6,1664]{2,1,0:T(8,128)(2,1)} %copy.193), calls=%async_computation.3 | async-start | bytes 425984 | tf_op jit(solution)/shard_map/all_to_all | solution.py:137
  276.1 10.0 %copy-start.17 = (f32[32,1664]{1,0:T(8,128)S(1)}, f32[32,1664]{1,0:T(8,128)}, u32[]{:S(2)}) copy-start(f32[32,1664]{1,0:T(8,128)} %convert_element_type.126) | copy-start | bytes 638980
  276.1 10.0 %copy-start.21 = (f32[32,2]{0,1:T(2,128)S(1)}, f32[32,2]{0,1:T(2,128)}, u32[]{:S(2)}) copy-start(f32[32,2]{0,1:T(2,128)} %param.8) | copy-start | bytes 772
  (8 other events, 13.3 us)
Sparse Core Ops, SparseCore 0:
  12.3 24.5 all-gather.2
  40.1 61.3 all-gather.4
  139.5 34.5 reduce-scatter.8
  177.3 35.7 reduce-scatter.4
  215.4 25.3 reduce-scatter.10
  243.2 24.1 reduce-scatter.6
where the time goes:
time: 295 us; the launch traced here: 294 us
  waiting for transfers between devices  92.5 us (31%)
  local copies, waits for them, and re-layouts  66.8 us (23%)
  matrix products  38.5 us (13%)
  blocking collectives  34.3 us (12%)
  other arithmetic  29.4 us (10%)
  between operations  16.5 us (6%)
  starting transfers between devices  16 us (5%)
    reduce_scatter x4, waiting for transfers between devices, scatter_axes(): shard = lax.psum_scatter(shard, axis, scatter_dimension=dim, tiled=True)  49.5 us
    all_gather x1, waiting for transfers between devices, sent_together(): lax.all_gather(both, axis, axis=dim, tiled=True)  37.2 us
    all_to_all x1, blocking collectives, in_one_piece(): lax.all_to_all(both, axis, split_axis=split_dim, concat_axis=concat_dim,...  23.6 us
    unnamed x53, local copies, waits for them, and re-layouts  14.6 us
    all_to_all x2, starting transfers between devices, settle_slots(): return lax.all_to_all(narrow, 'ex', split_axis=0, concat_axis=0, tiled=True)  11.8 us
    another operation x6, local copies, waits for them, and re-layouts  10.9 us
    all_to_all x1, blocking collectives, sum_at_owner(): lax.all_to_all(blocks, axis, split_axis=0, concat_axis=0, tiled=True)  10.6 us
    dot_general x2, matrix products, expert_backward(): jnp.einsum('arsjcbf,jdbf->arsjcbd', blocks, weight_parts, preferred_eleme...  7.31 us
  transfers between devices with their start and end apart: 9, of which 7 were waited for; matrix products, arithmetic and copies ran while one was open for 30% of the time, Pallas kernels for 0%

commit v1 on v0

v1 whole, which is shorter than its diff:
```python
import functools

import jax
import jax.numpy as jnp
import numpy as np
from jax import lax
from jax.experimental import pallas as pl
from jax.experimental.pallas import tpu as pltpu
from jax.sharding import PartitionSpec as P

MESH = pl.DeviceIdType.MESH
SIDE = 4
UNITS = SIDE * SIDE
FRAME = 16
SLOTS = 6
DELTAS = (0, -1, 1, 2)
F32 = jnp.float32
BF16 = jnp.bfloat16
gelu_scale = 0.7978845608028654


def pack_matrix(groups):
    single, doubled = 2 * groups, 4 * groups
    out = np.zeros((2 * (single + doubled), groups * FRAME), np.float32)
    for kind in range(2):
        for r in range(single):
            out[kind * (single + doubled) + r, (r // 2) * FRAME + kind * SLOTS + r % 2] = 1
        for r in range(doubled):
            out[kind * (single + doubled) + single + r, (r // 4) * FRAME + kind * SLOTS + 2 + r % 4] = 1
    return out


def column_tiles(width, step):
    return [(c, min(step, width - c)) for c in range(0, width, step)]


def layer_kernel(
    groups, copies_ref, select_ref, pack_ref, tokens_ref, cot_ref, gates_ref, wi_hbm, wo_hbm,
    layer_ref, gtok_ref, ggate_ref, gi_own_hbm, gi_got_hbm, go_own_hbm, go_got_hbm,
    wi, wo, frames, zin, xr, part, rbuf, own, frames_back, zback, hid, slope_v, dgelu, gi_v, go_v,
    w_send, w_recv, w_load, z_send, z_recv, ag_send, ag_recv, rs_send, rs_recv, zb_send, zb_recv, g_send, g_recv, g_store,
):
    width = tokens_ref.shape[1]
    hidden = wi.shape[3]
    et = lax.axis_index("et")
    ex = lax.axis_index("ex")
    dp = lax.axis_index("dp")
    y, x = lax.div(et, SIDE), lax.rem(et, SIDE)
    other = 1 - dp
    kind_rows = 6 * groups
    single = 2 * groups
    half_cut = (width // 128 + 1) // 2 * 128
    doubled = jnp.where(copies_ref[2 * ex + 1] == 2, 1, 0)

    def step_of(v, d):
        return lax.rem(v + (d + SIDE), SIDE)

    def unit_of(h, b, a):
        return b * SIDE + a if h == 0 else a * SIDE + b

    barrier = pltpu.get_barrier_semaphore()
    for dev in (
        unit_of(0, y, step_of(x, 1)), unit_of(0, y, step_of(x, -1)),
        unit_of(0, step_of(y, 1), x), unit_of(0, step_of(y, -1), x),
    ):
        pl.semaphore_signal(barrier, inc=1, device_id={"et": dev}, device_id_type=MESH)
    for o in range(1, groups):
        pl.semaphore_signal(barrier, inc=1, device_id={"ex": lax.rem(ex + o, groups)}, device_id_type=MESH)
    pl.semaphore_signal(barrier, inc=1, device_id={"dp": other}, device_id_type=MESH)

    loads = [
        pltpu.make_async_copy(wi_hbm, wi.at[0], w_load.at[0]),
        pltpu.make_async_copy(wo_hbm, wo.at[0], w_load.at[1]),
    ]
    for c in loads:
        c.start()

    cot = cot_ref[...].astype(F32)
    up0 = (cot * gates_ref[:, 0:1]).astype(BF16)
    up1 = (cot * gates_ref[:, 1:2]).astype(BF16)
    stacked = jnp.concatenate([tokens_ref[...], up0, up1], axis=0)
    made = jnp.dot(select_ref[...], stacked, preferred_element_type=F32).astype(BF16)
    frames[...] = made.reshape(groups, FRAME, width)

    pl.semaphore_wait(barrier, 4 + groups - 1 + 1)

    def z_copy(o, src, dst, send, recv):
        peer = lax.rem(ex + o, groups)
        return pltpu.make_async_remote_copy(
            src_ref=src.at[peer], dst_ref=dst.at[ex], send_sem=send, recv_sem=recv.at[ex],
            device_id={"ex": peer}, device_id_type=MESH,
        )

    def z_exchange(src, dst, send, recv):
        for o in range(1, groups):
            z_copy(o, src, dst, send, recv).start()
        dst[ex] = src[ex]

    def z_arrived(src, dst, send, recv):
        for o in range(1, groups):
            peer = lax.rem(ex + o, groups)
            pltpu.make_async_copy(src.at[peer], dst.at[peer], recv.at[peer]).wait()
        pltpu.make_async_copy(src.at[pl.ds(0, groups - 1)], dst.at[pl.ds(0, groups - 1)], send).wait()

    z_exchange(frames, zin, z_send, z_recv)
    swaps = [
        pltpu.make_async_remote_copy(
            src_ref=hbm, dst_ref=v.at[1], send_sem=w_send.at[i], recv_sem=w_recv.at[i],
            device_id={"dp": other}, device_id_type=MESH,
        )
        for i, (hbm, v) in enumerate(((wi_hbm, wi), (wo_hbm, wo)))
    ]
    for c in swaps:
        c.start()
    z_arrived(frames, zin, z_send, z_recv)

    def halves(h):
        return (x, y, 0, half_cut) if h == 0 else (y, x, half_cut, width - half_cut)

    def part_rows(k, p):
        cut = single if k == 0 else 2 * single
        return (0, cut) if p == 0 else (cut, kind_rows - cut)

    class Gather:
        def __init__(self, k, h):
            self.k, self.h = k, h
            self.a, self.b, self.c0, self.cn = halves(h)

        def ref(self, u, r0=0, rn=None):
            rn = kind_rows if rn is None else rn
            return xr.at[u, pl.ds(self.k * kind_rows + r0, rn), pl.ds(self.c0, self.cn)]

        def unit(self, db, da):
            return unit_of(self.h, step_of(self.b, db), step_of(self.a, da))

        def send(self, u, db, da, ident, rows=(0, None)):
            ref = self.ref(u, *rows)
            pltpu.make_async_remote_copy(
                src_ref=ref, dst_ref=ref, send_sem=ag_send, recv_sem=ag_recv.at[self.k, self.h, ident],
                device_id={"et": self.unit(db, da)}, device_id_type=MESH,
            ).start()

        def wait(self, u, ident, rows=(0, None)):
            ref = self.ref(u, *rows)
            pltpu.make_async_copy(ref, ref, ag_recv.at[self.k, self.h, ident]).wait()

        def start(self):
            u = self.unit(0, 0)
            self.send(u, 0, 1, 0)
            self.send(u, 0, -1, 1)
            self.send(u, 1, 0, 4)
            self.send(u, -1, 0, 8)

        def near(self):
            u = self.unit(0, -1)
            self.wait(u, 0)
            self.send(u, 0, 1, 2, part_rows(self.k, 0))
            self.send(u, 1, 0, 5)
            self.send(u, -1, 0, 9)
            u = self.unit(0, 1)
            self.wait(u, 1)
            self.send(u, 0, -1, 3, part_rows(self.k, 1))
            self.send(u, 1, 0, 6)
            self.send(u, -1, 0, 10)

        def far(self):
            u = self.unit(0, 2)
            self.wait(u, 2, part_rows(self.k, 0))
            self.wait(u, 3, part_rows(self.k, 1))
            self.send(u, 1, 0, 7)
            self.send(u, -1, 0, 11)

        def cross(self):
            for j, d in enumerate(DELTAS):
                u = self.unit(-1, d)
                self.wait(u, 4 + j)
                if j < 2:
                    self.send(u, 1, 0, 12 + j)
                u = self.unit(1, d)
                self.wait(u, 8 + j)
                if j >= 2:
                    self.send(u, -1, 0, 12 + j)

        def last(self):
            for j, d in enumerate(DELTAS):
                self.wait(self.unit(2, d), 12 + j)

    packed = jnp.dot(pack_ref[...], zin[...].reshape(groups * FRAME, width), preferred_element_type=F32)
    xr[et] = packed.astype(BF16)

    g_in = [Gather(0, h) for h in range(2)]
    g_up = [Gather(1, h) for h in range(2)]
    for g in g_in:
        g.start()
    for g in g_in:
        g.near()
    for g in g_up:
        g.start()
    for g in g_in:
        g.far()
    for g in g_up:
        g.near()
    for g in g_in:
        g.cross()
    for g in g_up:
        g.far()
    for g in g_in:
        g.last()
    for g in g_up:
        g.cross()
    for g in g_up:
        g.last()
    for c in loads:
        c.wait()
    for c in swaps:
        c.wait()

    half_units = UNITS // 2
    chunks = [
        (1 - doubled, 0, UNITS, 0, single, 0),
        (doubled, 0, half_units, single, 2 * single, UNITS * single),
        (doubled, half_units, half_units, single, 2 * single, 2 * UNITS * single),
    ]
    rows = UNITS * single
    tiles = column_tiles(width, 256)
    full_tiles = width // 256

    def over_tiles(body):
        def step(i, carry):
            body(pl.multiple_of(i * 256, 256), 256)
            return carry

        lax.fori_loop(0, full_tiles, step, 0)
        if width % 256:
            body(full_tiles * 256, width % 256)

    def block(ref, chunk, kind, c0=None, cn=None):
        _, u0, un, r0, rn, _ = chunk
        cols = slice(None) if c0 is None else pl.ds(c0, cn)
        return ref[pl.ds(u0, un), pl.ds(kind * kind_rows + r0, rn), cols].reshape(un * rn, width if c0 is None else cn)

    def put(ref, chunk, kind, c0, cn, value):
        _, u0, un, r0, rn, _ = chunk
        ref[pl.ds(u0, un), pl.ds(kind * kind_rows + r0, rn), pl.ds(c0, cn)] = value.reshape(un, rn, cn)

    for chunk in chunks:
        e, at = chunk[0], chunk[5]
        for q in range(2):
            v = jnp.dot(block(xr, chunk, 0), wi[q, e], preferred_element_type=F32)
            square = v * v
            t = jnp.tanh(gelu_scale * (v + 0.044715 * square * v))
            hid[pl.ds(at, rows), q * hidden:(q + 1) * hidden] = (0.5 * v * (1.0 + t)).astype(BF16)
            dgelu[pl.ds(at, rows), q * hidden:(q + 1) * hidden] = 0.5 * (1.0 + t) + 0.5 * v * (1.0 - t * t) * (
                gelu_scale * (1.0 + 3 * 0.044715 * square)
            )

    for chunk in chunks:
        e, at = chunk[0], chunk[5]

        def out_tile(c0, cn, chunk=chunk, e=e, at=at):
            total = jnp.dot(hid[pl.ds(at, rows), 0:hidden], wo[0, e, :, pl.ds(c0, cn)], preferred_element_type=F32)
            total += jnp.dot(hid[pl.ds(at, rows), hidden:2 * hidden], wo[1, e, :, pl.ds(c0, cn)], preferred_element_type=F32)
            put(part, chunk, 1, c0, cn, total.astype(BF16))

        over_tiles(out_tile)

    class Scatter:
        def __init__(self, k, h):
            self.k, self.h = k, h
            self.a, self.b, self.c0, self.cn = halves(h)

        def ref(self, u, r0=0, rn=None):
            rn = kind_rows if rn is None else rn
            return part.at[u, pl.ds(self.k * kind_rows + r0, rn), pl.ds(self.c0, self.cn)]

        def buf(self, slot, r0=0, rn=None):
            rn = kind_rows if rn is None else rn
            return rbuf.at[self.k, slot, pl.ds(r0, rn), pl.ds(self.c0, self.cn)]

        def unit(self, db, da):
            return unit_of(self.h, step_of(self.b, db), step_of(self.a, da))

        def send(self, u, db, da, slot, ident, rows=(0, None)):
            pltpu.make_async_remote_copy(
                src_ref=self.ref(u, *rows), dst_ref=self.buf(slot, *rows), send_sem=rs_send,
                recv_sem=rs_recv.at[self.k, self.h, ident],
                device_id={"et": self.unit(db, da)}, device_id_type=MESH,
            ).start()

        def wait(self, slot, ident, rows=(0, None)):
            ref = self.buf(slot, *rows)
            pltpu.make_async_copy(ref, ref, rs_recv.at[self.k, self.h, ident]).wait()

        def add(self, u, slots, rows=(0, None)):
            ref = self.ref(u, *rows)
            total = ref[...].astype(F32)
            for s in slots:
                total += self.buf(s, *rows)[...].astype(F32)
            ref[...] = total.astype(BF16)

        def start(self):
            for j, d in enumerate(DELTAS):
                self.send(self.unit(2, d), 1 if j < 2 else -1, 0, j, j)
            for j, d in enumerate(DELTAS):
                if j < 2:
                    self.send(self.unit(-1, d), -1, 0, 8 + j, 8 + j)
                else:
                    self.send(self.unit(1, d), 1, 0, 4 + j, 4 + j)

        def near(self):
            for j, d in enumerate(DELTAS):
                side = 1 if j < 2 else -1
                u = self.unit(side, d)
                self.wait(j, j)
                self.add(u, (j,))
                ident = (4 if j < 2 else 8) + j
                self.send(u, side, 0, ident, ident)

        def cross(self):
            for j in (3, 1, 2, 0):
                u = self.unit(0, DELTAS[j])
                self.wait(4 + j, 4 + j)
                self.wait(8 + j, 8 + j)
                self.add(u, (4 + j, 8 + j))
                if j == 3:
                    self.send(u, 0, 1, 12, 12, part_rows(self.k, 0))
                    self.send(u, 0, -1, 12, 13, part_rows(self.k, 1))

        def far(self):
            for p, side in ((0, 1), (1, -1)):
                u = self.unit(0, side)
                piece = part_rows(self.k, p)
                self.wait(12, 12 + p, piece)
                self.add(u, (12,), piece)
                self.send(u, 0, side, 13 + p, 14 + p)

        def last(self):
            self.wait(13, 14)
            self.wait(14, 15)
            total = self.ref(self.unit(0, 0))[...].astype(F32)
            for s in (13, 14):
                total += self.buf(s)[...].astype(F32)
            own[pl.ds(self.k * kind_rows, kind_rows), pl.ds(self.c0, self.cn)] = total.astype(BF16)

    s_in = [Scatter(0, h) for h in range(2)]
    s_out = [Scatter(1, h) for h in range(2)]
    for s in s_out:
        s.start()

    for chunk in chunks:
        e, at = chunk[0], chunk[5]
        for q in range(2):
            back = lax.dot_general(block(xr, chunk, 1), wo[q, e], (((1,), (1,)), ((), ())), preferred_element_type=F32)
            slope_v[pl.ds(at, rows), q * hidden:(q + 1) * hidden] = (
                back * dgelu[pl.ds(at, rows), q * hidden:(q + 1) * hidden]
            ).astype(BF16)

    for s in s_out:
        s.near()

    for chunk in chunks:
        e, at = chunk[0], chunk[5]

        def grad_tile(c0, cn, chunk=chunk, e=e, at=at):
            total = None
            for q in range(2):
                term = lax.dot_general(
                    slope_v[pl.ds(at, rows), q * hidden:(q + 1) * hidden], wi[q, e, pl.ds(c0, cn), :],
                    (((1,), (1,)), ((), ())), preferred_element_type=F32,
                )
                total = term if total is None else total + term
            put(part, chunk, 0, c0, cn, total.astype(BF16))

        over_tiles(grad_tile)

    for s in s_in:
        s.start()
    for s in s_out:
        s.cross()

    first_doubled = doubled == 0

    def tn(lhs, rhs):
        return lax.dot_general(lhs, rhs, (((0,), (0,)), ((), ())), preferred_element_type=F32)

    def whole(kind, role, c0, cn):
        r0, rn = (0, single) if role == 0 else (single, 2 * single)
        return xr[:, pl.ds(kind * kind_rows + r0, rn), pl.ds(c0, cn)].reshape(UNITS * rn, cn)

    def role_rows(ref, role):
        return ref[0:rows, :] if role == 0 else ref[rows:3 * rows, :]

    def gi_tile(c0, cn):
        by_role = [tn(whole(0, role, c0, cn), role_rows(slope_v, role)) for role in range(2)]
        for e in range(2):
            value = jnp.where(first_doubled, by_role[1 - e], by_role[e]).astype(BF16)
            for q in range(2):
                gi_v[q, e, pl.ds(c0, cn), :] = value[:, q * hidden:(q + 1) * hidden]

    def go_tile(c0, cn):
        by_role = [tn(role_rows(hid, role), whole(1, role, c0, cn)) for role in range(2)]
        for e in range(2):
            value = jnp.where(first_doubled, by_role[1 - e], by_role[e]).astype(BF16)
            for q in range(2):
                go_v[q, e, :, pl.ds(c0, cn)] = value[q * hidden:(q + 1) * hidden, :]

    def give(i, v, own_hbm, got_hbm):
        store = pltpu.make_async_copy(v.at[0], own_hbm, g_store.at[i])
        swap = pltpu.make_async_remote_copy(
            src_ref=v.at[1], dst_ref=got_hbm, send_sem=g_send.at[i], recv_sem=g_recv.at[i],
            device_id={"dp": other}, device_id_type=MESH,
        )
        store.start()
        swap.start()
        return store, swap

    over_tiles(go_tile)
    given = [give(0, go_v, go_own_hbm, go_got_hbm)]
    for s in s_out:
        s.far()
    for s in s_in:
        s.near()
    over_tiles(gi_tile)
    given.append(give(1, gi_v, gi_own_hbm, gi_got_hbm))
    for s in s_out:
        s.last()
    for s in s_in:
        s.cross()
    for s in s_in:
        s.far()
    for s in s_in:
        s.last()

    frames_back[...] = tn(pack_ref[...], own[...]).astype(BF16).reshape(groups, FRAME, width)
    z_exchange(frames_back, zback, zb_send, zb_recv)
    z_arrived(frames_back, zback, zb_send, zb_recv)
    result = tn(select_ref[...], zback[...].reshape(groups * FRAME, width))
    count = tokens_ref.shape[0]
    gtok_ref[...] = result[0:count].astype(BF16)
    first, second = result[count:2 * count], result[2 * count:3 * count]
    layer_ref[...] = (gates_ref[:, 0:1] * first + gates_ref[:, 1:2] * second).astype(BF16)
    ggate_ref[:, 0:1] = jnp.sum(cot * first, axis=1, keepdims=True)
    ggate_ref[:, 1:2] = jnp.sum(cot * second, axis=1, keepdims=True)

    sent = xr.at[pl.ds(0, UNITS - 1)]
    pltpu.make_async_copy(sent, sent, ag_send).wait()
    sent = part.at[pl.ds(0, UNITS - 1)]
    pltpu.make_async_copy(sent, sent, rs_send).wait()
    for store, swap in given:
        store.wait()
        swap.wait()


def selection(expert_ids, copies, groups):
    count = expert_ids.shape[0]
    pair = jnp.arange(2 * groups, dtype=jnp.int32)
    spots = jnp.arange(groups * FRAME, dtype=jnp.int32)[:, None]
    order = jnp.arange(count, dtype=jnp.int32)
    earlier = order[None, :] < order[:, None]
    places = []
    for k in range(2):
        ids = expert_ids[:, k]
        same = (ids[:, None] == expert_ids[None, :, 0]).astype(jnp.int32) + (
            ids[:, None] == expert_ids[None, :, 1]
        ).astype(jnp.int32)
        rank = jnp.sum(jnp.where(earlier, same, 0), axis=1)
        held = jnp.sum(jnp.where(ids[:, None] == pair[None, :], copies[None, :], 0), axis=1)
        spot = (ids // 2) * FRAME + jnp.where(held == 2, 2 + rank, rank)
        places.append(jnp.where(rank < 2 * held, spot, -FRAME))
    first, second = places
    token_rows = (spots == first[None, :]) | (spots == second[None, :])
    return jnp.concatenate(
        [token_rows, spots == first[None, :] + SLOTS, spots == second[None, :] + SLOTS], axis=1
    ).astype(BF16)


def shards(mesh_shape, tokens, gate_probs, expert_ids, copies, weight_in, weight_out, cotangent):
    groups = mesh_shape["ex"]
    count, width = tokens.shape
    hidden = weight_in.shape[2]
    unit_rows = 12 * groups
    kind_rows = 6 * groups
    all_rows = UNITS * kind_rows
    select = selection(expert_ids, copies, groups)
    pack = jnp.asarray(pack_matrix(groups), BF16)
    vmem, anywhere = pl.BlockSpec(memory_space=pltpu.VMEM), pl.BlockSpec(memory_space=pl.ANY)
    shape = jax.ShapeDtypeStruct
    dma = pltpu.SemaphoreType.DMA
    results = pl.pallas_call(
        functools.partial(layer_kernel, groups),
        out_shape=(
            shape((count, width), BF16), shape((count, width), BF16), shape((count, 2), F32),
            shape(weight_in.shape, BF16), shape(weight_in.shape, BF16),
            shape(weight_out.shape, BF16), shape(weight_out.shape, BF16),
        ),
        in_specs=[pl.BlockSpec(memory_space=pltpu.SMEM), vmem, vmem, vmem, vmem, vmem, anywhere, anywhere],
        out_specs=(vmem, vmem, vmem, anywhere, anywhere, anywhere, anywhere),
        scratch_shapes=[
            pltpu.VMEM((2,) + weight_in.shape, BF16),
            pltpu.VMEM((2,) + weight_out.shape, BF16),
            pltpu.VMEM((groups, FRAME, width), BF16),
            pltpu.VMEM((groups, FRAME, width), BF16),
            pltpu.VMEM((UNITS, unit_rows, width), BF16),
            pltpu.VMEM((UNITS, unit_rows, width), BF16),
            pltpu.VMEM((2, 15, kind_rows, width), BF16),
            pltpu.VMEM((unit_rows, width), BF16),
            pltpu.VMEM((groups, FRAME, width), BF16),
            pltpu.VMEM((groups, FRAME, width), BF16),
            pltpu.VMEM((all_rows, 2 * hidden), BF16),
            pltpu.VMEM((all_rows, 2 * hidden), BF16),
            pltpu.VMEM((all_rows, 2 * hidden), F32),
            pltpu.VMEM((2,) + weight_in.shape, BF16),
            pltpu.VMEM((2,) + weight_out.shape, BF16),
            dma((2,)), dma((2,)), dma((2,)),
            dma(()), dma((groups,)),
            dma(()), dma((2, 2, 16)),
            dma(()), dma((2, 2, 16)),
            dma(()), dma((groups,)),
            dma((2,)), dma((2,)), dma((2,)),
        ],
        compiler_params=pltpu.CompilerParams(
            collective_id=0, has_side_effects=True, vmem_limit_bytes=60 * 2**20
        ),
        name="moe_layer",
    )(copies, select, pack, tokens, cotangent, gate_probs, weight_in, weight_out)
    layer_out, grad_tokens, grad_gates, gi_own, gi_got, go_own, go_got = results
    return (
        layer_out,
        grad_tokens,
        grad_gates,
        gi_own.astype(F32) + gi_got.astype(F32),
        go_own.astype(F32) + go_got.astype(F32),
    )


def solution(mesh):
    rows = P(("et", "ex", "dp"), None)
    w_in = P("ex", None, ("et", "dp"))
    w_out = P("ex", ("et", "dp"), None)
    return jax.shard_map(
        functools.partial(shards, dict(mesh.shape)),
        mesh=mesh,
        in_specs=(rows, rows, rows, P(), w_in, w_out, rows),
        out_specs=(rows, rows, rows, w_in, w_out),
        check_vma=False,
    )
```

time: 295 us -> 120 us (0.41)
  Pallas kernels: 0 us -> 105 us
  waiting for transfers between devices: 92.5 us -> 0 us
  local copies, waits for them, and re-layouts: 66.8 us -> 4.78 us
  matrix products: 38.5 us -> 0 us
  blocking collectives: 34.3 us -> 0 us
  other arithmetic: 29.4 us -> 8.79 us
  starting transfers between devices: 16 us -> 0 us
  between operations: 16.5 us -> 0.67 us
    pallas_call x0 -> x1, Pallas kernels: none -> 105 us  [shards(): pl.pallas_call(functools.partial(layer_kernel, groups), out_shape=(shape(...]
    reduce_scatter x4 -> x0, waiting for transfers between devices: 49.5 us -> none  [scatter_axes(): shard = lax.psum_scatter(shard, axis, scatter_dimension=dim, tiled=True)]
    dot_general x16 -> x0, matrix products: 38.5 us -> none  [the longest x2 7.31 us: expert_backward(): jnp.einsum('arsjcbf,jdbf->arsjcbd', blocks, weight_parts, preferred_eleme...]
    all_gather x2 -> x0, waiting for transfers between devices: 37.2 us -> none  [the longest x1 37.2 us: sent_together(): lax.all_gather(both, axis, axis=dim, tiled=True)]
    all_to_all x2 -> x0, blocking collectives: 34.3 us -> none  [the longest x1 23.6 us: in_one_piece(): lax.all_to_all(both, axis, split_axis=split_dim, concat_axis=concat_dim,...]
    reduce_sum x8 -> x2, other arithmetic: 18.5 us -> 0.93 us  [the longest x1 0.75 us: selection(): jnp.sum(jnp.where(ids[:, None] == pair[None, :], copies[None, :], 0), axi...]
    all_to_all x3 -> x0, starting transfers between devices: 15.8 us -> none  [the longest x2 11.8 us: settle_slots(): return lax.all_to_all(narrow, 'ex', split_axis=0, concat_axis=0, tiled=True)]
    convert_element_type x6 -> x0, local copies, waits for them, and re-layouts: 12.2 us -> none  [the longest x2 6.65 us: shards(): part_in.astype(jnp.bfloat16)]
  transfers between devices with their start and end apart: 9 -> 0, of which waited for: 7 -> 0; matrix products, arithmetic and copies ran while one was open for 30% -> 0% of each run, Pallas kernels for 0% -> 0%
where the time goes in v1:
time: 120 us; the launch traced here: 119 us
  Pallas kernels  105 us (88%)
  other arithmetic  8.79 us (7%)
  local copies, waits for them, and re-layouts  4.78 us (4%)
    pallas_call x1, Pallas kernels, shards(): pl.pallas_call(functools.partial(layer_kernel, groups), out_shape=(shape(...  105 us
    add x1, other arithmetic, shards(): gi_own.astype(F32) + gi_got.astype(F32)  4.24 us
    unnamed x12, local copies, waits for them, and re-layouts  4.02 us

profile of v1, /device:TPU:8, one launch (start us, length us, event | category | flops | bytes accessed | tf_op | source)
XLA Modules:
  0.0 119.2 jit_solution(9453936871043797674)
XLA Ops:
  0.6 0.8 slice_bitcast_fusion.1
  1.4 0.2 select_reduce_fusion.1
  1.6 0.7 select_reduce_fusion.3
  2.3 0.8 broadcast_add_fusion.1
  3.1 1.4 %copy.15.gates_ref = f32[32,2]{1,0:T(8,128)} copy(f32[32,2]{0,1:T(2,128)} %param.9) | data formatting | bytes 512 | tf_op args[1]
  4.5 0.7 add_convert_fusion.select_ref
  5.2 104.9 %moe_layer.1 = (bf16[32,1664]{1,0:T(8,128)(2,1)}, bf16[32,1664]{1,0:T(8,128)(2,1)}, f32[32,2]{1,0:T(8,128)}, bf16[2,1664,256]{2,1,0:T(8,128)(2,1)}, bf16[2,1664,...) custom-call(s32[16]{0:T(128)} %copies_ref.1, ...), custom_call_target="tpu_custom_call" | custom-call | tf_op jit(solution)/shard_map/moe_layer/pallas_call | solution.py:489
  110.2 1.4 %copy.16 = f32[32,2]{0,1:T(2,128)} copy(f32[32,2]{1,0:T(8,128)} %get-tuple-element.26) | data formatting | bytes 512
  111.5 0.0 copy-start
  111.5 0.0 copy-start.1
  111.5 4.2 %convert_add_fusion.1 = f32[2,1664,256]{2,1,0:T(8,128)} fusion(bf16[2,1664,256]{2,1,0:T(8,128)(2,1)} %get-tuple-element.16, bf16[2,1664,256]{2,1,0:T(8,128)(2,1)} %get-tuple-element.15), kind=kLoop, calls=%fused_computation.1 | loop fusion | flops 2555904 | bytes 6815744 | tf_op jit(solution)/shard_map/add | solution.py:531
  115.8 0.0 copy-done
  115.8 0.0 copy-done.1
  115.8 0.0 copy-start.3
  115.8 0.0 copy-start.2
  115.8 2.1 %convert_add_fusion = f32[2,256,1664]{2,1,0:T(8,128)} fusion(bf16[2,256,1664]{2,1,0:T(8,128)(2,1)S(1)} %copy-done.1, bf16[2,256,1664]{2,1,0:T(8,128)(2,1)S(1)} %copy-done), kind=kLoop, calls=%fused_computation | loop fusion | flops 2555904 | bytes 6815744 | tf_op jit(solution)/shard_map/add | solution.py:532
  117.9 0.0 copy-done.3
  117.9 0.6 copy.19
  118.5 0.0 copy-done.2
  118.5 0.6 copy.20
  (2 shorter events, 0.0 us)
Async XLA Ops:
  111.5 4.3 %copy-start = (bf16[2,256,1664]{2,1,0:T(8,128)(2,1)S(1)}, bf16[2,256,1664]{2,1,0:T(8,128)(2,1)}, u32[]{:S(2)}) copy-start(bf16[2,256,1664]{2,1,0:T(8,128)(2,1)} %get-tuple-element.17) | copy-start | bytes 5111812
  111.5 4.3 %copy-start.1 = (bf16[2,256,1664]{2,1,0:T(8,128)(2,1)S(1)}, bf16[2,256,1664]{2,1,0:T(8,128)(2,1)}, u32[]{:S(2)}) copy-start(bf16[2,256,1664]{2,1,0:T(8,128)(2,1)} %get-tuple-element.18) | copy-start | bytes 5111812
  115.8 2.1 %copy-start.3 = (bf16[32,1664]{1,0:T(8,128)(2,1)S(1)}, bf16[32,1664]{1,0:T(8,128)(2,1)}, u32[]{:S(2)}) copy-start(bf16[32,1664]{1,0:T(8,128)(2,1)} %get-tuple-element.48) | copy-start | bytes 319492
  115.8 2.7 %copy-start.2 = (bf16[32,1664]{1,0:T(8,128)(2,1)S(1)}, bf16[32,1664]{1,0:T(8,128)(2,1)}, u32[]{:S(2)}) copy-start(bf16[32,1664]{1,0:T(8,128)(2,1)} %get-tuple-element.49) | copy-start | bytes 319492

commit v2 on v1

--- a/solution.py
+++ b/solution.py
@@ -11,8 +11,7 @@
 MESH = pl.DeviceIdType.MESH
 SIDE = 4
 UNITS = SIDE * SIDE
-FRAME = 16
-SLOTS = 6
+FRAME = 8
 DELTAS = (0, -1, 1, 2)
 F32 = jnp.float32
 BF16 = jnp.bfloat16
@@ -20,13 +19,12 @@
 
 
 def pack_matrix(groups):
-    single, doubled = 2 * groups, 4 * groups
-    out = np.zeros((2 * (single + doubled), groups * FRAME), np.float32)
-    for kind in range(2):
-        for r in range(single):
-            out[kind * (single + doubled) + r, (r // 2) * FRAME + kind * SLOTS + r % 2] = 1
-        for r in range(doubled):
-            out[kind * (single + doubled) + single + r, (r // 4) * FRAME + kind * SLOTS + 2 + r % 4] = 1
+    single = 2 * groups
+    out = np.zeros((3 * single, groups * FRAME), np.float32)
+    for r in range(single):
+        out[r, (r // 2) * FRAME + r % 2] = 1
+    for r in range(2 * single):
+        out[single + r, (r // 4) * FRAME + 2 + r % 4] = 1
     return out
 
 
@@ -35,10 +33,10 @@
 
 
 def layer_kernel(
-    groups, copies_ref, select_ref, pack_ref, tokens_ref, cot_ref, gates_ref, wi_hbm, wo_hbm,
+    groups, ids_hbm, copies_hbm, pack_hbm, tokens_hbm, cot_hbm, gates_hbm, wi_hbm, wo_hbm,
     layer_ref, gtok_ref, ggate_ref, gi_own_hbm, gi_got_hbm, go_own_hbm, go_got_hbm,
-    wi, wo, frames, zin, xr, part, rbuf, own, frames_back, zback, hid, slope_v, dgelu, gi_v, go_v,
-    w_send, w_recv, w_load, z_send, z_recv, ag_send, ag_recv, rs_send, rs_recv, zb_send, zb_recv, g_send, g_recv, g_store,
+    ids_ref, copies_ref, pack_ref, tokens_ref, cot_ref, gates_ref, wi, wo, frames, zin, xr, part, rbuf, own, frames_back, zback, hid, slope_v, dgelu, gi_v, go_v,
+    in_load, w_send, w_recv, w_load, z_send, z_recv, ag_send, ag_recv, rs_send, rs_recv, zb_send, zb_recv, g_send, g_recv, g_store,
 ):
     width = tokens_ref.shape[1]
     hidden = wi.shape[3]
@@ -50,13 +48,22 @@
     kind_rows = 6 * groups
     single = 2 * groups
     half_cut = (width // 128 + 1) // 2 * 128
-    doubled = jnp.where(copies_ref[2 * ex + 1] == 2, 1, 0)
 
     def step_of(v, d):
         return lax.rem(v + (d + SIDE), SIDE)
 
     def unit_of(h, b, a):
         return b * SIDE + a if h == 0 else a * SIDE + b
+
+    arrays = [
+        pltpu.make_async_copy(hbm, v, in_load.at[i])
+        for i, (hbm, v) in enumerate((
+            (ids_hbm, ids_ref), (copies_hbm, copies_ref), (gates_hbm, gates_ref),
+            (cot_hbm, cot_ref), (tokens_hbm, tokens_ref), (pack_hbm, pack_ref),
+        ))
+    ]
+    for c in arrays:
+        c.start()
 
     barrier = pltpu.get_barrier_semaphore()
     for dev in (
@@ -75,34 +82,63 @@
     for c in loads:
         c.start()
 
+    for c in arrays:
+        c.wait()
+    doubled = jnp.where(copies_ref[2 * ex + 1] == 2, 1, 0)
+    count = tokens_ref.shape[0]
+    square = (count, count)
+    down, along = lax.broadcasted_iota(jnp.int32, square, 0), lax.broadcasted_iota(jnp.int32, square, 1)
+    diagonal = down == along
+
+    def upright(row):
+        return jnp.sum(jnp.where(diagonal, jnp.broadcast_to(row, square), 0.0), axis=1, keepdims=True)
+
+    def lying(column):
+        return jnp.sum(jnp.where(diagonal, jnp.broadcast_to(column, square), 0.0), axis=0, keepdims=True)
+
+    ids = [ids_ref[k:k + 1, :] for k in range(2)]
+    columns = [upright(v.astype(F32)) for v in ids]
+    spots = lax.broadcasted_iota(jnp.int32, (groups * FRAME, count), 0)
+    chosen = []
+    for k in range(2):
+        mine = ids[k].astype(F32)
+        same = sum(jnp.where((c == mine) & (down < along), 1.0, 0.0) for c in columns)
+        rank = jnp.sum(same, axis=0, keepdims=True).astype(jnp.int32)
+        held = jnp.zeros_like(ids[k])
+        for e in range(2 * groups):
+            held = jnp.where(ids[k] == e, copies_ref[e], held)
+        spot = (ids[k] >> 1) * FRAME + jnp.where(held == 2, 2 + rank, rank)
+        spot = jnp.where(rank < 2 * held, spot, -1)
+        chosen.append(jnp.where(spots == spot, 1.0, 0.0).astype(BF16))
+    either = chosen[0] + chosen[1]
+    gates = [upright(gates_ref[k:k + 1, :]) for k in range(2)]
     cot = cot_ref[...].astype(F32)
-    up0 = (cot * gates_ref[:, 0:1]).astype(BF16)
-    up1 = (cot * gates_ref[:, 1:2]).astype(BF16)
-    stacked = jnp.concatenate([tokens_ref[...], up0, up1], axis=0)
-    made = jnp.dot(select_ref[...], stacked, preferred_element_type=F32).astype(BF16)
-    frames[...] = made.reshape(groups, FRAME, width)
+
+    def fill(kind, value):
+        frames[kind] = value.astype(BF16).reshape(groups, FRAME, width)
+
+    fill(0, jnp.dot(either, tokens_ref[...], preferred_element_type=F32))
+    fill(1, sum(jnp.dot(c, (cot * g).astype(BF16), preferred_element_type=F32) for c, g in zip(chosen, gates)))
 
     pl.semaphore_wait(barrier, 4 + groups - 1 + 1)
 
-    def z_copy(o, src, dst, send, recv):
-        peer = lax.rem(ex + o, groups)
-        return pltpu.make_async_remote_copy(
-            src_ref=src.at[peer], dst_ref=dst.at[ex], send_sem=send, recv_sem=recv.at[ex],
-            device_id={"ex": peer}, device_id_type=MESH,
-        )
-
-    def z_exchange(src, dst, send, recv):
-        for o in range(1, groups):
-            z_copy(o, src, dst, send, recv).start()
-        dst[ex] = src[ex]
-
-    def z_arrived(src, dst, send, recv):
+    def z_exchange(kind, src, dst, send, recv):
         for o in range(1, groups):
             peer = lax.rem(ex + o, groups)
-            pltpu.make_async_copy(src.at[peer], dst.at[peer], recv.at[peer]).wait()
-        pltpu.make_async_copy(src.at[pl.ds(0, groups - 1)], dst.at[pl.ds(0, groups - 1)], send).wait()
-
-    z_exchange(frames, zin, z_send, z_recv)
+            pltpu.make_async_remote_copy(
+                src_ref=src.at[kind, peer], dst_ref=dst.at[kind, ex], send_sem=send.at[kind], recv_sem=recv.at[kind, ex],
+                device_id={"ex": peer}, device_id_type=MESH,
+            ).start()
+        dst[kind, ex] = src[kind, ex]
+
+    def z_arrived(kind, src, dst, send, recv):
+        for o in range(1, groups):
+            peer = lax.rem(ex + o, groups)
+            pltpu.make_async_copy(src.at[kind, peer], dst.at[kind, peer], recv.at[kind, peer]).wait()
+        sent = src.at[kind, pl.ds(0, groups - 1)]
+        pltpu.make_async_copy(sent, sent, send.at[kind]).wait()
+
+    z_exchange(0, frames, zin, z_send, z_recv)
     swaps = [
         pltpu.make_async_remote_copy(
             src_ref=hbm, dst_ref=v.at[1], send_sem=w_send.at[i], recv_sem=w_recv.at[i],
@@ -110,9 +146,6 @@
         )
         for i, (hbm, v) in enumerate(((wi_hbm, wi), (wo_hbm, wo)))
     ]
-    for c in swaps:
-        c.start()
-    z_arrived(frames, zin, z_send, z_recv)
 
     def halves(h):
         return (x, y, 0, half_cut) if h == 0 else (y, x, half_cut, width - half_cut)
@@ -170,50 +203,31 @@
             self.send(u, 1, 0, 7)
             self.send(u, -1, 0, 11)
 
-        def cross(self):
-            for j, d in enumerate(DELTAS):
-                u = self.unit(-1, d)
-                self.wait(u, 4 + j)
-                if j < 2:
-                    self.send(u, 1, 0, 12 + j)
-                u = self.unit(1, d)
-                self.wait(u, 8 + j)
-                if j >= 2:
-                    self.send(u, -1, 0, 12 + j)
+        def cross(self, j):
+            d = DELTAS[j]
+            u = self.unit(-1, d)
+            self.wait(u, 4 + j)
+            if j < 2:
+                self.send(u, 1, 0, 12 + j)
+            u = self.unit(1, d)
+            self.wait(u, 8 + j)
+            if j >= 2:
+                self.send(u, -1, 0, 12 + j)
 
         def last(self):
             for j, d in enumerate(DELTAS):
                 self.wait(self.unit(2, d), 12 + j)
 
-    packed = jnp.dot(pack_ref[...], zin[...].reshape(groups * FRAME, width), preferred_element_type=F32)
-    xr[et] = packed.astype(BF16)
+    def unpack(kind):
+        rows_of_kind = jnp.dot(pack_ref[...], zin[kind].reshape(groups * FRAME, width), preferred_element_type=F32)
+        xr[et, pl.ds(kind * kind_rows, kind_rows), :] = rows_of_kind.astype(BF16)
 
     g_in = [Gather(0, h) for h in range(2)]
     g_up = [Gather(1, h) for h in range(2)]
-    for g in g_in:
-        g.start()
-    for g in g_in:
-        g.near()
-    for g in g_up:
-        g.start()
-    for g in g_in:
-        g.far()
-    for g in g_up:
-        g.near()
-    for g in g_in:
-        g.cross()
-    for g in g_up:
-        g.far()
-    for g in g_in:
-        g.last()
-    for g in g_up:
-        g.cross()
-    for g in g_up:
-        g.last()
-    for c in loads:
-        c.wait()
-    for c in swaps:
-        c.wait()
+
+    def each(movers, step, *args):
+        for m in movers:
+            getattr(m, step)(*args)
 
     half_units = UNITS // 2
     chunks = [
@@ -243,7 +257,7 @@
         _, u0, un, r0, rn, _ = chunk
         ref[pl.ds(u0, un), pl.ds(kind * kind_rows + r0, rn), pl.ds(c0, cn)] = value.reshape(un, rn, cn)
 
-    for chunk in chunks:
+    def forward_hidden(chunk):
         e, at = chunk[0], chunk[5]
         for q in range(2):
             v = jnp.dot(block(xr, chunk, 0), wi[q, e], preferred_element_type=F32)
@@ -254,15 +268,38 @@
                 gelu_scale * (1.0 + 3 * 0.044715 * square)
             )
 
-    for chunk in chunks:
+    def forward_out(chunk):
         e, at = chunk[0], chunk[5]
 
-        def out_tile(c0, cn, chunk=chunk, e=e, at=at):
+        def tile(c0, cn):
             total = jnp.dot(hid[pl.ds(at, rows), 0:hidden], wo[0, e, :, pl.ds(c0, cn)], preferred_element_type=F32)
             total += jnp.dot(hid[pl.ds(at, rows), hidden:2 * hidden], wo[1, e, :, pl.ds(c0, cn)], preferred_element_type=F32)
             put(part, chunk, 1, c0, cn, total.astype(BF16))
 
-        over_tiles(out_tile)
+        over_tiles(tile)
+
+    def backward_slope(chunk):
+        e, at = chunk[0], chunk[5]
+        for q in range(2):
+            back = lax.dot_general(block(xr, chunk, 1), wo[q, e], (((1,), (1,)), ((), ())), preferred_element_type=F32)
+            slope_v[pl.ds(at, rows), q * hidden:(q + 1) * hidden] = (
+                back * dgelu[pl.ds(at, rows), q * hidden:(q + 1) * hidden]
+            ).astype(BF16)
+
+    def backward_input(chunk):
+        e, at = chunk[0], chunk[5]
+
+        def tile(c0, cn):
+            total = sum(
+                lax.dot_general(
+                    slope_v[pl.ds(at, rows), q * hidden:(q + 1) * hidden], wi[q, e, pl.ds(c0, cn), :],
+                    (((1,), (1,)), ((), ())), preferred_element_type=F32,
+                )
+                for q in range(2)
+            )
+            put(part, chunk, 0, c0, cn, total.astype(BF16))
+
+        over_tiles(tile)
 
     class Scatter:
         def __init__(self, k, h):
@@ -307,24 +344,22 @@
                 else:
                     self.send(self.unit(1, d), 1, 0, 4 + j, 4 + j)
 
-        def near(self):
-            for j, d in enumerate(DELTAS):
-                side = 1 if j < 2 else -1
-                u = self.unit(side, d)
-                self.wait(j, j)
-                self.add(u, (j,))
-                ident = (4 if j < 2 else 8) + j
-                self.send(u, side, 0, ident, ident)
-
-        def cross(self):
-            for j in (3, 1, 2, 0):
-                u = self.unit(0, DELTAS[j])
-                self.wait(4 + j, 4 + j)
-                self.wait(8 + j, 8 + j)
-                self.add(u, (4 + j, 8 + j))
-                if j == 3:
-                    self.send(u, 0, 1, 12, 12, part_rows(self.k, 0))
-                    self.send(u, 0, -1, 12, 13, part_rows(self.k, 1))
+        def near(self, j):
+            side = 1 if j < 2 else -1
+            u = self.unit(side, DELTAS[j])
+            self.wait(j, j)
+            self.add(u, (j,))
+            ident = (4 if j < 2 else 8) + j
+            self.send(u, side, 0, ident, ident)
+
+        def cross(self, j):
+            u = self.unit(0, DELTAS[j])
+            self.wait(4 + j, 4 + j)
+            self.wait(8 + j, 8 + j)
+            self.add(u, (4 + j, 8 + j))
+            if j == 3:
+                self.send(u, 0, 1, 12, 12, part_rows(self.k, 0))
+                self.send(u, 0, -1, 12, 13, part_rows(self.k, 1))
 
         def far(self):
             for p, side in ((0, 1), (1, -1)):
@@ -344,40 +379,6 @@
 
     s_in = [Scatter(0, h) for h in range(2)]
     s_out = [Scatter(1, h) for h in range(2)]
-    for s in s_out:
-        s.start()
-
-    for chunk in chunks:
-        e, at = chunk[0], chunk[5]
-        for q in range(2):
-            back = lax.dot_general(block(xr, chunk, 1), wo[q, e], (((1,), (1,)), ((), ())), preferred_element_type=F32)
-            slope_v[pl.ds(at, rows), q * hidden:(q + 1) * hidden] = (
-                back * dgelu[pl.ds(at, rows), q * hidden:(q + 1) * hidden]
-            ).astype(BF16)
-
-    for s in s_out:
-        s.near()
-
-    for chunk in chunks:
-        e, at = chunk[0], chunk[5]
-
-        def grad_tile(c0, cn, chunk=chunk, e=e, at=at):
-            total = None
-            for q in range(2):
-                term = lax.dot_general(
-                    slope_v[pl.ds(at, rows), q * hidden:(q + 1) * hidden], wi[q, e, pl.ds(c0, cn), :],
-                    (((1,), (1,)), ((), ())), preferred_element_type=F32,
-                )
-                total = term if total is None else total + term
-            put(part, chunk, 0, c0, cn, total.astype(BF16))
-
-        over_tiles(grad_tile)
-
-    for s in s_in:
-        s.start()
-    for s in s_out:
-        s.cross()
-
     first_doubled = doubled == 0
 
     def tn(lhs, rhs):
@@ -414,33 +415,77 @@
         swap.start()
         return store, swap
 
+    def go_back(kind):
+        own_rows = own[pl.ds(kind * kind_rows, kind_rows), :]
+        frames_back[kind] = tn(pack_ref[...], own_rows).astype(BF16).reshape(groups, FRAME, width)
+        z_exchange(kind, frames_back, zback, zb_send, zb_recv)
+
+    def came_back(kind):
+        z_arrived(kind, frames_back, zback, zb_send, zb_recv)
+        return zback[kind].reshape(groups * FRAME, width)
+
+    z_arrived(0, frames, zin, z_send, z_recv)
+    unpack(0)
+    each(g_in, "start")
+    z_exchange(1, frames, zin, z_send, z_recv)
+    for c in swaps:
+        c.start()
+    each(g_in, "near")
+    z_arrived(1, frames, zin, z_send, z_recv)
+    unpack(1)
+    each(g_in, "far")
+    each(g_up, "start")
+    for j in range(4):
+        each(g_in, "cross", j)
+    each(g_up, "near")
+    for c in loads:
+        c.wait()
+    for c in swaps:
+        c.wait()
+    each(g_in, "last")
+    each(g_up, "far")
+    forward_hidden(chunks[0])
+    each(g_up, "cross", 0)
+    forward_hidden(chunks[1])
+    each(g_up, "cross", 1)
+    forward_hidden(chunks[2])
+    each(g_up, "cross", 2)
+    each(g_up, "cross", 3)
+    for c in chunks:
+        forward_out(c)
+    each(s_out, "start")
+    each(g_up, "last")
+    for j, c in enumerate(chunks):
+        backward_slope(c)
+    for j in (0, 2, 1, 3):
+        each(s_out, "near", j)
+    for c in chunks:
+        backward_input(c)
+    each(s_in, "start")
+    each(s_out, "cross", 3)
+    each(s_out, "cross", 1)
     over_tiles(go_tile)
     given = [give(0, go_v, go_own_hbm, go_got_hbm)]
-    for s in s_out:
-        s.far()
-    for s in s_in:
-        s.near()
+    each(s_out, "cross", 2)
+    each(s_out, "cross", 0)
+    each(s_out, "far")
+    for j in (0, 2, 1, 3):
+        each(s_in, "near", j)
+    each(s_out, "last")
+    go_back(1)
     over_tiles(gi_tile)
     given.append(give(1, gi_v, gi_own_hbm, gi_got_hbm))
-    for s in s_out:
-        s.last()
-    for s in s_in:
-        s.cross()
-    for s in s_in:
-        s.far()
-    for s in s_in:
-        s.last()
-
-    frames_back[...] = tn(pack_ref[...], own[...]).astype(BF16).reshape(groups, FRAME, width)
-    z_exchange(frames_back, zback, zb_send, zb_recv)
-    z_arrived(frames_back, zback, zb_send, zb_recv)
-    result = tn(select_ref[...], zback[...].reshape(groups * FRAME, width))
-    count = tokens_ref.shape[0]
-    gtok_ref[...] = result[0:count].astype(BF16)
-    first, second = result[count:2 * count], result[2 * count:3 * count]
-    layer_ref[...] = (gates_ref[:, 0:1] * first + gates_ref[:, 1:2] * second).astype(BF16)
-    ggate_ref[:, 0:1] = jnp.sum(cot * first, axis=1, keepdims=True)
-    ggate_ref[:, 1:2] = jnp.sum(cot * second, axis=1, keepdims=True)
+    for j in (3, 1, 2, 0):
+        each(s_in, "cross", j)
+    each(s_in, "far")
+    back = came_back(1)
+    first, second = tn(chosen[0], back), tn(chosen[1], back)
+    layer_ref[...] = (gates[0] * first + gates[1] * second).astype(BF16)
+    ggate_ref[0:1, :] = lying(jnp.sum(cot * first, axis=1, keepdims=True))
+    ggate_ref[1:2, :] = lying(jnp.sum(cot * second, axis=1, keepdims=True))
+    each(s_in, "last")
+    go_back(0)
+    gtok_ref[...] = tn(either, came_back(0)).astype(BF16)
 
     sent = xr.at[pl.ds(0, UNITS - 1)]
     pltpu.make_async_copy(sent, sent, ag_send).wait()
@@ -451,29 +496,6 @@
         swap.wait()
 
 
-def selection(expert_ids, copies, groups):
-    count = expert_ids.shape[0]
-    pair = jnp.arange(2 * groups, dtype=jnp.int32)
-    spots = jnp.arange(groups * FRAME, dtype=jnp.int32)[:, None]
-    order = jnp.arange(count, dtype=jnp.int32)
-    earlier = order[None, :] < order[:, None]
-    places = []
-    for k in range(2):
-        ids = expert_ids[:, k]
-        same = (ids[:, None] == expert_ids[None, :, 0]).astype(jnp.int32) + (
-            ids[:, None] == expert_ids[None, :, 1]
-        ).astype(jnp.int32)
-        rank = jnp.sum(jnp.where(earlier, same, 0), axis=1)
-        held = jnp.sum(jnp.where(ids[:, None] == pair[None, :], copies[None, :], 0), axis=1)
-        spot = (ids // 2) * FRAME + jnp.where(held == 2, 2 + rank, rank)
-        places.append(jnp.where(rank < 2 * held, spot, -FRAME))
-    first, second = places
-    token_rows = (spots == first[None, :]) | (spots == second[None, :])
-    return jnp.concatenate(
-        [token_rows, spots == first[None, :] + SLOTS, spots == second[None, :] + SLOTS], axis=1
-    ).astype(BF16)
-
-
 def shards(mesh_shape, tokens, gate_probs, expert_ids, copies, weight_in, weight_out, cotangent):
     groups = mesh_shape["ex"]
     count, width = tokens.shape
@@ -481,7 +503,6 @@
     unit_rows = 12 * groups
     kind_rows = 6 * groups
     all_rows = UNITS * kind_rows
-    select = selection(expert_ids, copies, groups)
     pack = jnp.asarray(pack_matrix(groups), BF16)
     vmem, anywhere = pl.BlockSpec(memory_space=pltpu.VMEM), pl.BlockSpec(memory_space=pl.ANY)
     shape = jax.ShapeDtypeStruct
@@ -489,45 +510,50 @@
     results = pl.pallas_call(
         functools.partial(layer_kernel, groups),
         out_shape=(
-            shape((count, width), BF16), shape((count, width), BF16), shape((count, 2), F32),
+            shape((count, width), BF16), shape((count, width), BF16), shape((2, count), F32),
             shape(weight_in.shape, BF16), shape(weight_in.shape, BF16),
             shape(weight_out.shape, BF16), shape(weight_out.shape, BF16),
         ),
-        in_specs=[pl.BlockSpec(memory_space=pltpu.SMEM), vmem, vmem, vmem, vmem, vmem, anywhere, anywhere],
+        in_specs=[pl.BlockSpec(memory_space=pltpu.HBM)] * 8,
         out_specs=(vmem, vmem, vmem, anywhere, anywhere, anywhere, anywhere),
         scratch_shapes=[
+            pltpu.VMEM((2, count), jnp.int32), pltpu.SMEM(copies.shape, jnp.int32), pltpu.VMEM(pack.shape, BF16),
+            pltpu.VMEM((count, width), BF16), pltpu.VMEM((count, width), BF16), pltpu.VMEM((2, count), F32),
             pltpu.VMEM((2,) + weight_in.shape, BF16),
             pltpu.VMEM((2,) + weight_out.shape, BF16),
-            pltpu.VMEM((groups, FRAME, width), BF16),
-            pltpu.VMEM((groups, FRAME, width), BF16),
+            pltpu.VMEM((2, groups, FRAME, width), BF16),
+            pltpu.VMEM((2, groups, FRAME, width), BF16),
             pltpu.VMEM((UNITS, unit_rows, width), BF16),
             pltpu.VMEM((UNITS, unit_rows, width), BF16),
             pltpu.VMEM((2, 15, kind_rows, width), BF16),
             pltpu.VMEM((unit_rows, width), BF16),
-            pltpu.VMEM((groups, FRAME, width), BF16),
-            pltpu.VMEM((groups, FRAME, width), BF16),
+            pltpu.VMEM((2, groups, FRAME, width), BF16),
+            pltpu.VMEM((2, groups, FRAME, width), BF16),
             pltpu.VMEM((all_rows, 2 * hidden), BF16),
             pltpu.VMEM((all_rows, 2 * hidden), BF16),
             pltpu.VMEM((all_rows, 2 * hidden), F32),
             pltpu.VMEM((2,) + weight_in.shape, BF16),
             pltpu.VMEM((2,) + weight_out.shape, BF16),
-            dma((2,)), dma((2,)), dma((2,)),
-            dma(()), dma((groups,)),
+            dma((6,)), dma((2,)), dma((2,)), dma((2,)),
+            dma((2,)), dma((2, groups)),
             dma(()), dma((2, 2, 16)),
             dma(()), dma((2, 2, 16)),
-            dma(()), dma((groups,)),
+            dma((2,)), dma((2, groups)),
             dma((2,)), dma((2,)), dma((2,)),
         ],
         compiler_params=pltpu.CompilerParams(
-            collective_id=0, has_side_effects=True, vmem_limit_bytes=60 * 2**20
+            collective_id=0, has_side_effects=True, vmem_limit_bytes=46 * 2**20
         ),
         name="moe_layer",
-    )(copies, select, pack, tokens, cotangent, gate_probs, weight_in, weight_out)
+    )(*(
+        pltpu.with_memory_space_constraint(v, pltpu.HBM)
+        for v in (expert_ids.T, copies, pack, tokens, cotangent, gate_probs.T, weight_in, weight_out)
+    ))
     layer_out, grad_tokens, grad_gates, gi_own, gi_got, go_own, go_got = results
     return (
         layer_out,
         grad_tokens,
-        grad_gates,
+        grad_gates.T,
         gi_own.astype(F32) + gi_got.astype(F32),
         go_own.astype(F32) + go_got.astype(F32),
     )

time: 120 us -> 102 us (0.85)
  Pallas kernels: 105 us -> 95.3 us
  other arithmetic: 8.79 us -> 4.21 us
  local copies, waits for them, and re-layouts: 4.78 us -> 1.85 us
    pallas_call x1, Pallas kernels: 105 us -> 95.3 us  [shards(): pl.pallas_call(functools.partial(layer_kernel, groups), out_shape=(shape(...]
    unnamed x12 -> x3, local copies, waits for them, and re-layouts: 4.02 us -> 1.85 us
    add x1, other arithmetic: 4.24 us -> 2.13 us  [shards(): gi_own.astype(F32) + gi_got.astype(F32)]
where the time goes in v2:
time: 102 us
  Pallas kernels  95.3 us (93%)
  other arithmetic  4.21 us (4%)
  local copies, waits for them, and re-layouts  1.85 us (2%)
    pallas_call x1, Pallas kernels, shards(): pl.pallas_call(functools.partial(layer_kernel, groups), out_shape=(shape(...  95.3 us
    add x1, other arithmetic, shards(): gi_own.astype(F32) + gi_got.astype(F32)  2.13 us
    add x1, other arithmetic, shards(): go_own.astype(F32) + go_got.astype(F32)  2.08 us

profile of v2, /device:TPU:8, one launch (start us, length us, event | category | flops | bytes accessed | tf_op | source)
XLA Modules:
  0.0 102.0 jit_solution(7110889625603546829)
XLA Ops:
  0.6 95.3 %moe_layer.1 = (bf16[32,1664]{1,0:T(8,128)(2,1)S(1)}, bf16[32,1664]{1,0:T(8,128)(2,1)S(1)}, f32[2,32]{1,0:T(2,128)S(1)}, bf16[2,1664,256]{2,1,0:T(8,128)(2,1)S(1...) custom-call(s32[2,32]{1,0:T(2,128)} %bitcast.4, ...), custom_call_target="tpu_custom_call" | custom-call | tf_op jit(solution)/shard_map/moe_layer/pallas_call | solution.py:510
  95.9 2.1 %convert_add_fusion.1 = f32[2,1664,256]{2,1,0:T(8,128)} fusion(bf16[2,1664,256]{2,1,0:T(8,128)(2,1)S(1)} %get-tuple-element.16, bf16[2,1664,256]{2,1,0:T(8,128)(2,1)S(1)} %get-tuple-element.15), kind=kLoop, calls=%fused_computation.1 | loop fusion | flops 2555904 | bytes 6815744 | tf_op jit(solution)/shard_map/add | solution.py:557
  98.1 2.1 %convert_add_fusion = f32[2,256,1664]{2,1,0:T(8,128)} fusion(bf16[2,256,1664]{2,1,0:T(8,128)(2,1)S(1)} %get-tuple-element.18, bf16[2,256,1664]{2,1,0:T(8,128)(2,1)S(1)} %get-tuple-element.17), kind=kLoop, calls=%fused_computation | loop fusion | flops 2555904 | bytes 6815744 | tf_op jit(solution)/shard_map/add | solution.py:558
  100.1 0.6 copy.16
  100.8 0.6 copy.17
  101.4 0.6 copy.18

commit v3 on v2

--- a/solution.py
+++ b/solution.py
@@ -122,23 +122,29 @@
 
     pl.semaphore_wait(barrier, 4 + groups - 1 + 1)
 
-    def z_exchange(kind, src, dst, send, recv):
+    spans = ((0, half_cut), (half_cut, width - half_cut))
+
+    def z_exchange(kind, h, src, dst, send, recv):
+        cols = pl.ds(*spans[h])
         for o in range(1, groups):
             peer = lax.rem(ex + o, groups)
             pltpu.make_async_remote_copy(
-                src_ref=src.at[kind, peer], dst_ref=dst.at[kind, ex], send_sem=send.at[kind], recv_sem=recv.at[kind, ex],
+                src_ref=src.at[kind, peer, :, cols], dst_ref=dst.at[kind, ex, :, cols],
+                send_sem=send.at[kind, h], recv_sem=recv.at[kind, h, ex],
                 device_id={"ex": peer}, device_id_type=MESH,
             ).start()
-        dst[kind, ex] = src[kind, ex]
-
-    def z_arrived(kind, src, dst, send, recv):
+        dst[kind, ex, :, cols] = src[kind, ex, :, cols]
+
+    def z_arrived(kind, h, src, dst, send, recv):
+        cols = pl.ds(*spans[h])
         for o in range(1, groups):
             peer = lax.rem(ex + o, groups)
-            pltpu.make_async_copy(src.at[kind, peer], dst.at[kind, peer], recv.at[kind, peer]).wait()
-        sent = src.at[kind, pl.ds(0, groups - 1)]
-        pltpu.make_async_copy(sent, sent, send.at[kind]).wait()
-
-    z_exchange(0, frames, zin, z_send, z_recv)
+            pltpu.make_async_copy(src.at[kind, peer, :, cols], dst.at[kind, peer, :, cols], recv.at[kind, h, peer]).wait()
+        sent = src.at[kind, pl.ds(0, groups - 1), :, cols]
+        pltpu.make_async_copy(sent, sent, send.at[kind, h]).wait()
+
+    for h in range(2):
+        z_exchange(0, h, frames, zin, z_send, z_recv)
     swaps = [
         pltpu.make_async_remote_copy(
             src_ref=hbm, dst_ref=v.at[1], send_sem=w_send.at[i], recv_sem=w_recv.at[i],
@@ -147,8 +153,9 @@
         for i, (hbm, v) in enumerate(((wi_hbm, wi), (wo_hbm, wo)))
     ]
 
-    def halves(h):
-        return (x, y, 0, half_cut) if h == 0 else (y, x, half_cut, width - half_cut)
+    def halves(k, h):
+        a, b = (x, y) if h == k else (y, x)
+        return (a, b) + spans[h]
 
     def part_rows(k, p):
         cut = single if k == 0 else 2 * single
@@ -157,14 +164,14 @@
     class Gather:
         def __init__(self, k, h):
             self.k, self.h = k, h
-            self.a, self.b, self.c0, self.cn = halves(h)
+            self.a, self.b, self.c0, self.cn = halves(k, h)
 
         def ref(self, u, r0=0, rn=None):
             rn = kind_rows if rn is None else rn
             return xr.at[u, pl.ds(self.k * kind_rows + r0, rn), pl.ds(self.c0, self.cn)]
 
         def unit(self, db, da):
-            return unit_of(self.h, step_of(self.b, db), step_of(self.a, da))
+            return unit_of(self.h ^ self.k, step_of(self.b, db), step_of(self.a, da))
 
         def send(self, u, db, da, ident, rows=(0, None)):
             ref = self.ref(u, *rows)
@@ -218,9 +225,12 @@
             for j, d in enumerate(DELTAS):
                 self.wait(self.unit(2, d), 12 + j)
 
-    def unpack(kind):
-        rows_of_kind = jnp.dot(pack_ref[...], zin[kind].reshape(groups * FRAME, width), preferred_element_type=F32)
-        xr[et, pl.ds(kind * kind_rows, kind_rows), :] = rows_of_kind.astype(BF16)
+    def unpack(kind, h):
+        cols = pl.ds(*spans[h])
+        z_arrived(kind, h, frames, zin, z_send, z_recv)
+        frame_rows = zin[kind, :, :, cols].reshape(groups * FRAME, spans[h][1])
+        unit_rows = jnp.dot(pack_ref[...], frame_rows, preferred_element_type=F32)
+        xr[et, pl.ds(kind * kind_rows, kind_rows), cols] = unit_rows.astype(BF16)
 
     g_in = [Gather(0, h) for h in range(2)]
     g_up = [Gather(1, h) for h in range(2)]
@@ -304,7 +314,7 @@
     class Scatter:
         def __init__(self, k, h):
             self.k, self.h = k, h
-            self.a, self.b, self.c0, self.cn = halves(h)
+            self.a, self.b, self.c0, self.cn = halves(k, h)
 
         def ref(self, u, r0=0, rn=None):
             rn = kind_rows if rn is None else rn
@@ -315,7 +325,7 @@
             return rbuf.at[self.k, slot, pl.ds(r0, rn), pl.ds(self.c0, self.cn)]
 
         def unit(self, db, da):
-            return unit_of(self.h, step_of(self.b, db), step_of(self.a, da))
+            return unit_of(self.h ^ self.k, step_of(self.b, db), step_of(self.a, da))
 
         def send(self, u, db, da, slot, ident, rows=(0, None)):
             pltpu.make_async_remote_copy(
@@ -336,9 +346,11 @@
             ref[...] = total.astype(BF16)
 
         def start(self):
-            for j, d in enumerate(DELTAS):
-                self.send(self.unit(2, d), 1 if j < 2 else -1, 0, j, j)
-            for j, d in enumerate(DELTAS):
+            order = (3, 1, 2, 0)
+            for j in order:
+                self.send(self.unit(2, DELTAS[j]), 1 if j < 2 else -1, 0, j, j)
+            for j in order:
+                d = DELTAS[j]
                 if j < 2:
                     self.send(self.unit(-1, d), -1, 0, 8 + j, 8 + j)
                 else:
@@ -415,77 +427,102 @@
         swap.start()
         return store, swap
 
-    def go_back(kind):
-        own_rows = own[pl.ds(kind * kind_rows, kind_rows), :]
-        frames_back[kind] = tn(pack_ref[...], own_rows).astype(BF16).reshape(groups, FRAME, width)
-        z_exchange(kind, frames_back, zback, zb_send, zb_recv)
-
-    def came_back(kind):
-        z_arrived(kind, frames_back, zback, zb_send, zb_recv)
-        return zback[kind].reshape(groups * FRAME, width)
-
-    z_arrived(0, frames, zin, z_send, z_recv)
-    unpack(0)
-    each(g_in, "start")
-    z_exchange(1, frames, zin, z_send, z_recv)
+    def go_back(kind, h):
+        cols = pl.ds(*spans[h])
+        own_rows = own[pl.ds(kind * kind_rows, kind_rows), cols]
+        frames_back[kind, :, :, cols] = tn(pack_ref[...], own_rows).astype(BF16).reshape(groups, FRAME, spans[h][1])
+        z_exchange(kind, h, frames_back, zback, zb_send, zb_recv)
+
+    def came_back(kind, h):
+        z_arrived(kind, h, frames_back, zback, zb_send, zb_recv)
+        return zback[kind, :, :, pl.ds(*spans[h])].reshape(groups * FRAME, spans[h][1])
+
+    def finish_out():
+        dots = [0.0, 0.0]
+        for h in range(2):
+            cols = pl.ds(*spans[h])
+            back = came_back(1, h)
+            pair = [tn(c, back) for c in chosen]
+            layer_ref[:, cols] = (gates[0] * pair[0] + gates[1] * pair[1]).astype(BF16)
+            part_cot = cot_ref[:, cols].astype(F32)
+            dots = [d + jnp.sum(part_cot * p, axis=1, keepdims=True) for d, p in zip(dots, pair)]
+        for k in range(2):
+            ggate_ref[k:k + 1, :] = lying(dots[k])
+
+    unpack(0, 0)
+    g_in[0].start()
+    unpack(0, 1)
+    g_in[1].start()
+    for h in range(2):
+        z_exchange(1, h, frames, zin, z_send, z_recv)
     for c in swaps:
         c.start()
     each(g_in, "near")
-    z_arrived(1, frames, zin, z_send, z_recv)
-    unpack(1)
     each(g_in, "far")
-    each(g_up, "start")
-    for j in range(4):
-        each(g_in, "cross", j)
-    each(g_up, "near")
+    each(g_in, "cross", 0)
+    each(g_in, "cross", 1)
+    for h in range(2):
+        unpack(1, h)
+        g_up[h].start()
+    each(g_in, "cross", 2)
+    each(g_in, "cross", 3)
     for c in loads:
         c.wait()
     for c in swaps:
         c.wait()
     each(g_in, "last")
+    each(g_up, "near")
+    forward_hidden(chunks[0])
     each(g_up, "far")
-    forward_hidden(chunks[0])
+    forward_hidden(chunks[1])
+    forward_hidden(chunks[2])
     each(g_up, "cross", 0)
-    forward_hidden(chunks[1])
+    forward_out(chunks[0])
     each(g_up, "cross", 1)
-    forward_hidden(chunks[2])
+    forward_out(chunks[1])
     each(g_up, "cross", 2)
+    forward_out(chunks[2])
     each(g_up, "cross", 3)
-    for c in chunks:
-        forward_out(c)
     each(s_out, "start")
     each(g_up, "last")
-    for j, c in enumerate(chunks):
-        backward_slope(c)
-    for j in (0, 2, 1, 3):
-        each(s_out, "near", j)
-    for c in chunks:
-        backward_input(c)
+    backward_slope(chunks[0])
+    backward_slope(chunks[1])
+    each(s_out, "near", 3)
+    each(s_out, "near", 1)
+    backward_slope(chunks[2])
+    each(s_out, "near", 2)
+    each(s_out, "near", 0)
+    backward_input(chunks[0])
+    backward_input(chunks[1])
+    each(s_out, "cross", 3)
+    backward_input(chunks[2])
     each(s_in, "start")
-    each(s_out, "cross", 3)
     each(s_out, "cross", 1)
+    each(s_out, "cross", 2)
+    each(s_out, "far")
+    each(s_in, "near", 3)
+    each(s_in, "near", 1)
     over_tiles(go_tile)
     given = [give(0, go_v, go_own_hbm, go_got_hbm)]
-    each(s_out, "cross", 2)
     each(s_out, "cross", 0)
-    each(s_out, "far")
-    for j in (0, 2, 1, 3):
-        each(s_in, "near", j)
-    each(s_out, "last")
-    go_back(1)
+    each(s_in, "near", 2)
+    each(s_in, "near", 0)
+    for h in range(2):
+        s_out[h].last()
+        go_back(1, h)
+    each(s_in, "cross", 3)
+    each(s_in, "cross", 1)
+    each(s_in, "cross", 2)
+    each(s_in, "far")
     over_tiles(gi_tile)
     given.append(give(1, gi_v, gi_own_hbm, gi_got_hbm))
-    for j in (3, 1, 2, 0):
-        each(s_in, "cross", j)
-    each(s_in, "far")
-    back = came_back(1)
-    first, second = tn(chosen[0], back), tn(chosen[1], back)
-    layer_ref[...] = (gates[0] * first + gates[1] * second).astype(BF16)
-    ggate_ref[0:1, :] = lying(jnp.sum(cot * first, axis=1, keepdims=True))
-    ggate_ref[1:2, :] = lying(jnp.sum(cot * second, axis=1, keepdims=True))
-    each(s_in, "last")
-    go_back(0)
-    gtok_ref[...] = tn(either, came_back(0)).astype(BF16)
+    each(s_in, "cross", 0)
+    finish_out()
+    for h in range(2):
+        s_in[h].last()
+        go_back(0, h)
+    for h in range(2):
+        gtok_ref[:, pl.ds(*spans[h])] = tn(either, came_back(0, h)).astype(BF16)
 
     sent = xr.at[pl.ds(0, UNITS - 1)]
     pltpu.make_async_copy(sent, sent, ag_send).wait()
@@ -494,6 +531,28 @@
     for store, swap in given:
         store.wait()
         swap.wait()
+
+
+def finish_kernel(
+    layer_ref, gtok_ref, ggate_ref, gi_own, gi_got, go_own, go_got,
+    layer_hbm, gtok_hbm, ggate_hbm, gi_hbm, go_hbm, gi_v, go_v, small_sem, sum_sem,
+):
+    copies = [
+        pltpu.make_async_copy(v, hbm, small_sem.at[i])
+        for i, (v, hbm) in enumerate(((layer_ref, layer_hbm), (gtok_ref, gtok_hbm), (ggate_ref, ggate_hbm)))
+    ]
+    for c in copies:
+        c.start()
+    for i, (own, got, total, hbm) in enumerate(((gi_own, gi_got, gi_v, gi_hbm), (go_own, go_got, go_v, go_hbm))):
+        piece = own.shape[1] // 4
+        for e in range(2):
+            for n in range(4):
+                here = (e, pl.ds(n * piece, piece))
+                total[here] = own[here].astype(F32) + got[here].astype(F32)
+                copies.append(pltpu.make_async_copy(total.at[here], hbm.at[here], sum_sem.at[i, e, n]))
+                copies[-1].start()
+    for c in copies:
+        c.wait()
 
 
 def shards(mesh_shape, tokens, gate_probs, expert_ids, copies, weight_in, weight_out, cotangent):
@@ -535,10 +594,10 @@
             pltpu.VMEM((2,) + weight_in.shape, BF16),
             pltpu.VMEM((2,) + weight_out.shape, BF16),
             dma((6,)), dma((2,)), dma((2,)), dma((2,)),
-            dma((2,)), dma((2, groups)),
+            dma((2, 2)), dma((2, 2, groups)),
             dma(()), dma((2, 2, 16)),
             dma(()), dma((2, 2, 16)),
-            dma((2,)), dma((2, groups)),
+            dma((2, 2)), dma((2, 2, groups)),
             dma((2,)), dma((2,)), dma((2,)),
         ],
         compiler_params=pltpu.CompilerParams(
@@ -549,14 +608,22 @@
         pltpu.with_memory_space_constraint(v, pltpu.HBM)
         for v in (expert_ids.T, copies, pack, tokens, cotangent, gate_probs.T, weight_in, weight_out)
     ))
-    layer_out, grad_tokens, grad_gates, gi_own, gi_got, go_own, go_got = results
-    return (
-        layer_out,
-        grad_tokens,
-        grad_gates.T,
-        gi_own.astype(F32) + gi_got.astype(F32),
-        go_own.astype(F32) + go_got.astype(F32),
-    )
+    hbm = pl.BlockSpec(memory_space=pltpu.HBM)
+    layer_out, grad_tokens, grad_gates, grad_in, grad_out = pl.pallas_call(
+        finish_kernel,
+        out_shape=(
+            shape((count, width), BF16), shape((count, width), BF16), shape((2, count), F32),
+            shape(weight_in.shape, F32), shape(weight_out.shape, F32),
+        ),
+        in_specs=[vmem] * 7,
+        out_specs=(hbm,) * 5,
+        scratch_shapes=[
+            pltpu.VMEM(weight_in.shape, F32), pltpu.VMEM(weight_out.shape, F32), dma((3,)), dma((2, 2, 4)),
+        ],
+        compiler_params=pltpu.CompilerParams(vmem_limit_bytes=8 * 2**20),
+        name="replica_sums",
+    )(*(pltpu.with_memory_space_constraint(v, pltpu.VMEM) for v in results))
+    return layer_out, grad_tokens, grad_gates.T, grad_in, grad_out
 
 
 def solution(mesh):

time: 102 us -> 93.6 us (0.918); the launches traced: 102 us -> 92.4 us
  other arithmetic: 4.21 us -> 0 us
  Pallas kernels: 95.3 us -> 91.7 us
  local copies, waits for them, and re-layouts: 1.85 us -> 0 us
    pallas_call x1, Pallas kernels: 95.3 us -> 88.7 us  [shards(): pl.pallas_call(functools.partial(layer_kernel, groups), out_shape=(shape(...]
    add x2 -> x0, other arithmetic: 4.21 us -> none  [the longest x1 2.13 us: shards(): gi_own.astype(F32) + gi_got.astype(F32)]
    pallas_call x0 -> x1, Pallas kernels: none -> 3.05 us  [shards(): pl.pallas_call(finish_kernel, out_shape=(shape((count, width), BF16), sha...]
    unnamed x3 -> x0, local copies, waits for them, and re-layouts: 1.85 us -> none
where the time goes in v3:
time: 93.6 us; the launch traced here: 92.4 us
  Pallas kernels  91.7 us (98%)
    pallas_call x1, Pallas kernels, shards(): pl.pallas_call(functools.partial(layer_kernel, groups), out_shape=(shape(...  88.7 us
    pallas_call x1, Pallas kernels, shards(): pl.pallas_call(finish_kernel, out_shape=(shape((count, width), BF16), sha...  3.05 us

profile of v3, /device:TPU:8, one launch (start us, length us, event | category | flops | bytes accessed | tf_op | source)
XLA Modules:
  0.0 92.4 jit_solution(7197760936391835098)
XLA Ops:
  0.6 88.7 %moe_layer.1 = (bf16[32,1664]{1,0:T(8,128)(2,1)S(1)}, bf16[32,1664]{1,0:T(8,128)(2,1)S(1)}, f32[2,32]{1,0:T(2,128)S(1)}, bf16[2,1664,256]{2,1,0:T(8,128)(2,1)S(1...) custom-call(s32[2,32]{1,0:T(2,128)} %bitcast.3, ...), custom_call_target="tpu_custom_call" | custom-call | tf_op jit(solution)/shard_map/moe_layer/pallas_call | solution.py:569
  89.3 3.1 %replica_sums.1 = (bf16[32,1664]{1,0:T(8,128)(2,1)}, bf16[32,1664]{1,0:T(8,128)(2,1)}, f32[2,32]{1,0:T(2,128)}, f32[2,1664,256]{2,1,0:T(8,128)}, f32[2,256,1664]{2,1,0:T(8,128)}) custom-call(bf16[32,1664]{1,0:T(8,128)(2,1)S(1)} %get-tuple-element.17.layer_ref, bf16[32,1664]{1,0:T(8,128)(2,1)S(1)} %get-tuple-element.18.gtok_ref, ...), custom_call_target="tpu_custom_call" | custom-call | tf_op jit(solution)/shard_map/replica_sums/pallas_call | solution.py:612

commit v4 on v3

--- a/solution.py
+++ b/solution.py
@@ -69,6 +69,7 @@
     for dev in (
         unit_of(0, y, step_of(x, 1)), unit_of(0, y, step_of(x, -1)),
         unit_of(0, step_of(y, 1), x), unit_of(0, step_of(y, -1), x),
+        unit_of(0, y, step_of(x, 2)), unit_of(0, step_of(y, 2), x),
     ):
         pl.semaphore_signal(barrier, inc=1, device_id={"et": dev}, device_id_type=MESH)
     for o in range(1, groups):
@@ -112,15 +113,6 @@
         chosen.append(jnp.where(spots == spot, 1.0, 0.0).astype(BF16))
     either = chosen[0] + chosen[1]
     gates = [upright(gates_ref[k:k + 1, :]) for k in range(2)]
-    cot = cot_ref[...].astype(F32)
-
-    def fill(kind, value):
-        frames[kind] = value.astype(BF16).reshape(groups, FRAME, width)
-
-    fill(0, jnp.dot(either, tokens_ref[...], preferred_element_type=F32))
-    fill(1, sum(jnp.dot(c, (cot * g).astype(BF16), preferred_element_type=F32) for c, g in zip(chosen, gates)))
-
-    pl.semaphore_wait(barrier, 4 + groups - 1 + 1)
 
     spans = ((0, half_cut), (half_cut, width - half_cut))
 
@@ -143,8 +135,22 @@
         sent = src.at[kind, pl.ds(0, groups - 1), :, cols]
         pltpu.make_async_copy(sent, sent, send.at[kind, h]).wait()
 
+    def fill(kind, h):
+        cols = pl.ds(*spans[h])
+        if kind == 0:
+            value = jnp.dot(either, tokens_ref[:, cols], preferred_element_type=F32)
+        else:
+            part_cot = cot_ref[:, cols].astype(F32)
+            value = sum(jnp.dot(c, (part_cot * g).astype(BF16), preferred_element_type=F32) for c, g in zip(chosen, gates))
+        frames[kind, :, :, cols] = value.astype(BF16).reshape(groups, FRAME, spans[h][1])
+
+    fill(0, 0)
+    pl.semaphore_wait(barrier, 6 + groups - 1 + 1)
+    z_exchange(0, 0, frames, zin, z_send, z_recv)
+    fill(0, 1)
+    z_exchange(0, 1, frames, zin, z_send, z_recv)
     for h in range(2):
-        z_exchange(0, h, frames, zin, z_send, z_recv)
+        fill(1, h)
     swaps = [
         pltpu.make_async_remote_copy(
             src_ref=hbm, dst_ref=v.at[1], send_sem=w_send.at[i], recv_sem=w_recv.at[i],
@@ -157,56 +163,49 @@
         a, b = (x, y) if h == k else (y, x)
         return (a, b) + spans[h]
 
-    def part_rows(k, p):
-        cut = single if k == 0 else 2 * single
-        return (0, cut) if p == 0 else (cut, kind_rows - cut)
-
     class Gather:
         def __init__(self, k, h):
             self.k, self.h = k, h
             self.a, self.b, self.c0, self.cn = halves(k, h)
 
-        def ref(self, u, r0=0, rn=None):
-            rn = kind_rows if rn is None else rn
-            return xr.at[u, pl.ds(self.k * kind_rows + r0, rn), pl.ds(self.c0, self.cn)]
+        def ref(self, u):
+            return xr.at[u, pl.ds(self.k * kind_rows, kind_rows), pl.ds(self.c0, self.cn)]
 
         def unit(self, db, da):
             return unit_of(self.h ^ self.k, step_of(self.b, db), step_of(self.a, da))
 
-        def send(self, u, db, da, ident, rows=(0, None)):
-            ref = self.ref(u, *rows)
+        def send(self, u, db, da, ident):
+            ref = self.ref(u)
             pltpu.make_async_remote_copy(
                 src_ref=ref, dst_ref=ref, send_sem=ag_send, recv_sem=ag_recv.at[self.k, self.h, ident],
                 device_id={"et": self.unit(db, da)}, device_id_type=MESH,
             ).start()
 
-        def wait(self, u, ident, rows=(0, None)):
-            ref = self.ref(u, *rows)
+        def wait(self, u, ident):
+            ref = self.ref(u)
             pltpu.make_async_copy(ref, ref, ag_recv.at[self.k, self.h, ident]).wait()
 
         def start(self):
             u = self.unit(0, 0)
             self.send(u, 0, 1, 0)
             self.send(u, 0, -1, 1)
+            self.send(u, 0, 2, 2)
             self.send(u, 1, 0, 4)
             self.send(u, -1, 0, 8)
 
         def near(self):
             u = self.unit(0, -1)
             self.wait(u, 0)
-            self.send(u, 0, 1, 2, part_rows(self.k, 0))
             self.send(u, 1, 0, 5)
             self.send(u, -1, 0, 9)
             u = self.unit(0, 1)
             self.wait(u, 1)
-            self.send(u, 0, -1, 3, part_rows(self.k, 1))
             self.send(u, 1, 0, 6)
             self.send(u, -1, 0, 10)
 
         def far(self):
             u = self.unit(0, 2)
-            self.wait(u, 2, part_rows(self.k, 0))
-            self.wait(u, 3, part_rows(self.k, 1))
+            self.wait(u, 2)
             self.send(u, 1, 0, 7)
             self.send(u, -1, 0, 11)
 
@@ -316,40 +315,40 @@
             self.k, self.h = k, h
             self.a, self.b, self.c0, self.cn = halves(k, h)
 
-        def ref(self, u, r0=0, rn=None):
-            rn = kind_rows if rn is None else rn
-            return part.at[u, pl.ds(self.k * kind_rows + r0, rn), pl.ds(self.c0, self.cn)]
-
-        def buf(self, slot, r0=0, rn=None):
-            rn = kind_rows if rn is None else rn
-            return rbuf.at[self.k, slot, pl.ds(r0, rn), pl.ds(self.c0, self.cn)]
+        def ref(self, u):
+            return part.at[u, pl.ds(self.k * kind_rows, kind_rows), pl.ds(self.c0, self.cn)]
+
+        def buf(self, slot):
+            return rbuf.at[self.k, slot, :, pl.ds(self.c0, self.cn)]
 
         def unit(self, db, da):
             return unit_of(self.h ^ self.k, step_of(self.b, db), step_of(self.a, da))
 
-        def send(self, u, db, da, slot, ident, rows=(0, None)):
+        def send(self, u, db, da, slot, ident):
             pltpu.make_async_remote_copy(
-                src_ref=self.ref(u, *rows), dst_ref=self.buf(slot, *rows), send_sem=rs_send,
+                src_ref=self.ref(u), dst_ref=self.buf(slot), send_sem=rs_send,
                 recv_sem=rs_recv.at[self.k, self.h, ident],
                 device_id={"et": self.unit(db, da)}, device_id_type=MESH,
             ).start()
 
-        def wait(self, slot, ident, rows=(0, None)):
-            ref = self.buf(slot, *rows)
+        def wait(self, slot, ident):
+            ref = self.buf(slot)
             pltpu.make_async_copy(ref, ref, rs_recv.at[self.k, self.h, ident]).wait()
 
-        def add(self, u, slots, rows=(0, None)):
-            ref = self.ref(u, *rows)
+        def add(self, u, slots):
+            ref = self.ref(u)
             total = ref[...].astype(F32)
             for s in slots:
-                total += self.buf(s, *rows)[...].astype(F32)
+                total += self.buf(s)[...].astype(F32)
             ref[...] = total.astype(BF16)
 
         def start(self):
             order = (3, 1, 2, 0)
             for j in order:
                 self.send(self.unit(2, DELTAS[j]), 1 if j < 2 else -1, 0, j, j)
-            for j in order:
+
+        def early(self):
+            for j in (3, 1, 2, 0):
                 d = DELTAS[j]
                 if j < 2:
                     self.send(self.unit(-1, d), -1, 0, 8 + j, 8 + j)
@@ -369,23 +368,14 @@
             self.wait(4 + j, 4 + j)
             self.wait(8 + j, 8 + j)
             self.add(u, (4 + j, 8 + j))
-            if j == 3:
-                self.send(u, 0, 1, 12, 12, part_rows(self.k, 0))
-                self.send(u, 0, -1, 12, 13, part_rows(self.k, 1))
-
-        def far(self):
-            for p, side in ((0, 1), (1, -1)):
-                u = self.unit(0, side)
-                piece = part_rows(self.k, p)
-                self.wait(12, 12 + p, piece)
-                self.add(u, (12,), piece)
-                self.send(u, 0, side, 13 + p, 14 + p)
+            if j:
+                place = {3: 12, 2: 13, 1: 14}[j]
+                self.send(u, 0, DELTAS[j], place, place)
 
         def last(self):
-            self.wait(13, 14)
-            self.wait(14, 15)
             total = self.ref(self.unit(0, 0))[...].astype(F32)
-            for s in (13, 14):
+            for s in (13, 14, 12):
+                self.wait(s, s)
                 total += self.buf(s)[...].astype(F32)
             own[pl.ds(self.k * kind_rows, kind_rows), pl.ds(self.c0, self.cn)] = total.astype(BF16)
 
@@ -484,6 +474,7 @@
     forward_out(chunks[2])
     each(g_up, "cross", 3)
     each(s_out, "start")
+    each(s_out, "early")
     each(g_up, "last")
     backward_slope(chunks[0])
     backward_slope(chunks[1])
@@ -497,9 +488,9 @@
     each(s_out, "cross", 3)
     backward_input(chunks[2])
     each(s_in, "start")
+    each(s_in, "early")
     each(s_out, "cross", 1)
     each(s_out, "cross", 2)
-    each(s_out, "far")
     each(s_in, "near", 3)
     each(s_in, "near", 1)
     over_tiles(go_tile)
@@ -513,7 +504,6 @@
     each(s_in, "cross", 3)
     each(s_in, "cross", 1)
     each(s_in, "cross", 2)
-    each(s_in, "far")
     over_tiles(gi_tile)
     given.append(give(1, gi_v, gi_own_hbm, gi_got_hbm))
     each(s_in, "cross", 0)

time: 93.6 us -> 91.6 us (0.979)
  Pallas kernels: 91.7 us -> 90.3 us
    pallas_call x1, Pallas kernels: 88.7 us -> 87.3 us  [shards(): pl.pallas_call(functools.partial(layer_kernel, groups), out_shape=(shape(...]
where the time goes in v4:
time: 91.6 us; the launch traced here: 90.9 us
  Pallas kernels  90.3 us (99%)
    pallas_call x1, Pallas kernels, shards(): pl.pallas_call(functools.partial(layer_kernel, groups), out_shape=(shape(...  87.3 us
    pallas_call x1, Pallas kernels, shards(): pl.pallas_call(finish_kernel, out_shape=(shape((count, width), BF16), sha...  3.05 us

profile of v4, /device:TPU:8, one launch (start us, length us, event | category | flops | bytes accessed | tf_op | source)
XLA Modules:
  0.0 90.9 jit_solution(8180291541906246736)
XLA Ops:
  0.6 87.3 %moe_layer.1 = (bf16[32,1664]{1,0:T(8,128)(2,1)S(1)}, bf16[32,1664]{1,0:T(8,128)(2,1)S(1)}, f32[2,32]{1,0:T(2,128)S(1)}, bf16[2,1664,256]{2,1,0:T(8,128)(2,1)S(1...) custom-call(s32[2,32]{1,0:T(2,128)} %bitcast.3, ...), custom_call_target="tpu_custom_call" | custom-call | tf_op jit(solution)/shard_map/moe_layer/pallas_call | solution.py:559
  87.9 3.1 %replica_sums.1 = (bf16[32,1664]{1,0:T(8,128)(2,1)}, bf16[32,1664]{1,0:T(8,128)(2,1)}, f32[2,32]{1,0:T(2,128)}, f32[2,1664,256]{2,1,0:T(8,128)}, f32[2,256,1664]{2,1,0:T(8,128)}) custom-call(bf16[32,1664]{1,0:T(8,128)(2,1)S(1)} %get-tuple-element.17.layer_ref, bf16[32,1664]{1,0:T(8,128)(2,1)S(1)} %get-tuple-element.18.gtok_ref, ...), custom_call_target="tpu_custom_call" | custom-call | tf_op jit(solution)/shard_map/replica_sums/pallas_call | solution.py:602

commit v5 on v4

--- a/solution.py
+++ b/solution.py
@@ -65,6 +65,9 @@
     for c in arrays:
         c.start()
 
+    zin[...] = jnp.zeros_like(zin)
+    zback[...] = jnp.zeros_like(zback)
+
     barrier = pltpu.get_barrier_semaphore()
     for dev in (
         unit_of(0, y, step_of(x, 1)), unit_of(0, y, step_of(x, -1)),
@@ -115,13 +118,14 @@
     gates = [upright(gates_ref[k:k + 1, :]) for k in range(2)]
 
     spans = ((0, half_cut), (half_cut, width - half_cut))
+    held_rows = pl.ds(0, 6)
 
     def z_exchange(kind, h, src, dst, send, recv):
         cols = pl.ds(*spans[h])
         for o in range(1, groups):
             peer = lax.rem(ex + o, groups)
             pltpu.make_async_remote_copy(
-                src_ref=src.at[kind, peer, :, cols], dst_ref=dst.at[kind, ex, :, cols],
+                src_ref=src.at[kind, peer, held_rows, cols], dst_ref=dst.at[kind, ex, held_rows, cols],
                 send_sem=send.at[kind, h], recv_sem=recv.at[kind, h, ex],
                 device_id={"ex": peer}, device_id_type=MESH,
             ).start()
@@ -131,8 +135,10 @@
         cols = pl.ds(*spans[h])
         for o in range(1, groups):
             peer = lax.rem(ex + o, groups)
-            pltpu.make_async_copy(src.at[kind, peer, :, cols], dst.at[kind, peer, :, cols], recv.at[kind, h, peer]).wait()
-        sent = src.at[kind, pl.ds(0, groups - 1), :, cols]
+            pltpu.make_async_copy(
+                src.at[kind, peer, held_rows, cols], dst.at[kind, peer, held_rows, cols], recv.at[kind, h, peer]
+            ).wait()
+        sent = src.at[kind, pl.ds(0, groups - 1), held_rows, cols]
         pltpu.make_async_copy(sent, sent, send.at[kind, h]).wait()
 
     def fill(kind, h):
@@ -507,10 +513,10 @@
     over_tiles(gi_tile)
     given.append(give(1, gi_v, gi_own_hbm, gi_got_hbm))
     each(s_in, "cross", 0)
-    finish_out()
     for h in range(2):
         s_in[h].last()
         go_back(0, h)
+    finish_out()
     for h in range(2):
         gtok_ref[:, pl.ds(*spans[h])] = tn(either, came_back(0, h)).astype(BF16)
 

time: 91.6 us -> 89 us (0.972)
  Pallas kernels: 90.3 us -> 88.3 us
    pallas_call x1, Pallas kernels: 87.3 us -> 85.2 us  [shards(): pl.pallas_call(functools.partial(layer_kernel, groups), out_shape=(shape(...]
where the time goes in v5:
time: 89 us; the launch traced here: 88.9 us
  Pallas kernels  88.3 us (99%)
    pallas_call x1, Pallas kernels, shards(): pl.pallas_call(functools.partial(layer_kernel, groups), out_shape=(shape(...  85.2 us
    pallas_call x1, Pallas kernels, shards(): pl.pallas_call(finish_kernel, out_shape=(shape((count, width), BF16), sha...  3.05 us

profile of v5, /device:TPU:8, one launch (start us, length us, event | category | flops | bytes accessed | tf_op | source)
XLA Modules:
  0.0 88.9 jit_solution(6866954626965238432)
XLA Ops:
  0.6 85.2 %moe_layer.1 = (bf16[32,1664]{1,0:T(8,128)(2,1)S(1)}, bf16[32,1664]{1,0:T(8,128)(2,1)S(1)}, f32[2,32]{1,0:T(2,128)S(1)}, bf16[2,1664,256]{2,1,0:T(8,128)(2,1)S(1...) custom-call(s32[2,32]{1,0:T(2,128)} %bitcast.3, ...), custom_call_target="tpu_custom_call" | custom-call | tf_op jit(solution)/shard_map/moe_layer/pallas_call | solution.py:565
  85.9 3.1 %replica_sums.1 = (bf16[32,1664]{1,0:T(8,128)(2,1)}, bf16[32,1664]{1,0:T(8,128)(2,1)}, f32[2,32]{1,0:T(2,128)}, f32[2,1664,256]{2,1,0:T(8,128)}, f32[2,256,1664]{2,1,0:T(8,128)}) custom-call(bf16[32,1664]{1,0:T(8,128)(2,1)S(1)} %get-tuple-element.17.layer_ref, bf16[32,1664]{1,0:T(8,128)(2,1)S(1)} %get-tuple-element.18.gtok_ref, ...), custom_call_target="tpu_custom_call" | custom-call | tf_op jit(solution)/shard_map/replica_sums/pallas_call | solution.py:608

commit v6 on v5

--- a/solution.py
+++ b/solution.py
@@ -447,10 +447,10 @@
 
     unpack(0, 0)
     g_in[0].start()
+    z_exchange(1, 0, frames, zin, z_send, z_recv)
     unpack(0, 1)
     g_in[1].start()
-    for h in range(2):
-        z_exchange(1, h, frames, zin, z_send, z_recv)
+    z_exchange(1, 1, frames, zin, z_send, z_recv)
     for c in swaps:
         c.start()
     each(g_in, "near")
@@ -478,9 +478,9 @@
     forward_out(chunks[1])
     each(g_up, "cross", 2)
     forward_out(chunks[2])
-    each(g_up, "cross", 3)
     each(s_out, "start")
     each(s_out, "early")
+    each(g_up, "cross", 3)
     each(g_up, "last")
     backward_slope(chunks[0])
     backward_slope(chunks[1])
@@ -504,12 +504,12 @@
     each(s_out, "cross", 0)
     each(s_in, "near", 2)
     each(s_in, "near", 0)
+    each(s_in, "cross", 3)
+    each(s_in, "cross", 1)
+    each(s_in, "cross", 2)
     for h in range(2):
         s_out[h].last()
         go_back(1, h)
-    each(s_in, "cross", 3)
-    each(s_in, "cross", 1)
-    each(s_in, "cross", 2)
     over_tiles(gi_tile)
     given.append(give(1, gi_v, gi_own_hbm, gi_got_hbm))
     each(s_in, "cross", 0)

time: 89 us -> 92.5 us (1.039)
  Pallas kernels: 88.3 us -> 91.8 us
    pallas_call x1, Pallas kernels: 85.2 us -> 88.7 us  [shards(): pl.pallas_call(functools.partial(layer_kernel, groups), out_shape=(shape(...]
where the time goes in v6:
time: 92.5 us; the launch traced here: 92.4 us
  Pallas kernels  91.8 us (99%)
    pallas_call x1, Pallas kernels, shards(): pl.pallas_call(functools.partial(layer_kernel, groups), out_shape=(shape(...  88.7 us
    pallas_call x1, Pallas kernels, shards(): pl.pallas_call(finish_kernel, out_shape=(shape((count, width), BF16), sha...  3.05 us

profile of v6, /device:TPU:8, one launch (start us, length us, event | category | flops | bytes accessed | tf_op | source)
XLA Modules:
  0.0 92.4 jit_solution(6053678315792751386)
XLA Ops:
  0.6 88.7 %moe_layer.1 = (bf16[32,1664]{1,0:T(8,128)(2,1)S(1)}, bf16[32,1664]{1,0:T(8,128)(2,1)S(1)}, f32[2,32]{1,0:T(2,128)S(1)}, bf16[2,1664,256]{2,1,0:T(8,128)(2,1)S(1...) custom-call(s32[2,32]{1,0:T(2,128)} %bitcast.3, ...), custom_call_target="tpu_custom_call" | custom-call | tf_op jit(solution)/shard_map/moe_layer/pallas_call | solution.py:565
  89.4 3.1 %replica_sums.1 = (bf16[32,1664]{1,0:T(8,128)(2,1)}, bf16[32,1664]{1,0:T(8,128)(2,1)}, f32[2,32]{1,0:T(2,128)}, f32[2,1664,256]{2,1,0:T(8,128)}, f32[2,256,1664]{2,1,0:T(8,128)}) custom-call(bf16[32,1664]{1,0:T(8,128)(2,1)S(1)} %get-tuple-element.17.layer_ref, bf16[32,1664]{1,0:T(8,128)(2,1)S(1)} %get-tuple-element.18.gtok_ref, ...), custom_call_target="tpu_custom_call" | custom-call | tf_op jit(solution)/shard_map/replica_sums/pallas_call | solution.py:608
